TPU v7x, 32 devices: a whole 2x2x4 slice. The times are simulated.
32 devices in a mesh: seq: 16 (over z, y, core), dp: 2 (over x).
Axes of the slice: x: 2, y: 2, z: 4, core: 2. Of those that a mesh axis runs over, the one named last changes fastest.
Arguments:
- tokens: bfloat16 [2, 2048, 1024], P('dp', 'seq'), may hold values from -6 to 6
- cotangent: bfloat16 [2, 2048, 1024], P('dp', 'seq'), may hold values from -6 to 6
- lengths: int32 [2], replicated, may hold values from 512 to 2048, as said below
- assign: int32 [2], replicated, may hold values from 0 to 1, each once
- w_qkv: bfloat16 [1024, 3072], P(('seq', 'dp')), may hold values from -0.1875 to 0.1875
- qv_bias: bfloat16 [2, 1024], P(None, ('seq', 'dp')), may hold values from -4 to 4
- w_out: bfloat16 [1024, 1024], P(('seq', 'dp')), may hold values from -1.5 to 1.5
- out_bias: bfloat16 [1024], P(('seq', 'dp')), may hold values from -1.5 to 1.5
- w_up: bfloat16 [1024, 4096], P(('seq', 'dp')), may hold values from -0.1875 to 0.1875
- up_bias: bfloat16 [4096], P(('seq', 'dp')), may hold values from -4 to 4
- w_down: bfloat16 [4096, 1024], P(('seq', 'dp')), may hold values from -0.09375 to 0.09375
- down_bias: bfloat16 [1024], P(('seq', 'dp')), may hold values from -3 to 3
- norm_gain: bfloat16 [4, 1024], P(None, ('seq', 'dp')), may hold values from 0.5 to 1.5
- norm_shift: bfloat16 [4, 1024], P(None, ('seq', 'dp')), may hold values from -4 to 4
Outputs:
- output: bfloat16 [2, 2048, 1024], P('dp', 'seq')
- input_grad: bfloat16 [2, 2048, 1024], P('dp', 'seq')
- grad_w_qkv: float32 [1024, 3072], P(('seq', 'dp'))
- grad_qv_bias: float32 [2, 1024], P(None, ('seq', 'dp'))
- grad_w_out: float32 [1024, 1024], P(('seq', 'dp'))
- grad_out_bias: float32 [1024], P(('seq', 'dp'))
- grad_w_up: float32 [1024, 4096], P(('seq', 'dp'))
- grad_up_bias: float32 [4096], P(('seq', 'dp'))
- grad_w_down: float32 [4096, 1024], P(('seq', 'dp'))
- grad_down_bias: float32 [1024], P(('seq', 'dp'))
- grad_norm_gain: float32 [4, 1024], P(None, ('seq', 'dp'))
- grad_norm_shift: float32 [4, 1024], P(None, ('seq', 'dp'))
Inputs may be any that keep to these rules, and one draw needn't show every extreme that they name: `lengths`: each sequence's valid positions; some sequence fills its whole slot of 2048. `assign`: every sequence stands in exactly one slot.
All inputs are finite; a program needn't handle non-finite values.
Results may differ from a plain program's by a relative error of at most 0.01.
Values may be sent and summed in bfloat16 or wider, within the bound.
A program may use at most 192 MiB of HBM per device.

v0:
```python
import functools
import math

import jax
import jax.numpy as jnp
from jax import lax
from jax.experimental import pallas as pl
from jax.experimental.pallas import tpu as pltpu
from jax.sharding import PartitionSpec as P


HD = 64


RELAX_SCALE = 32.0
NORM_EPSILON = 1e-05


def norm_rows(values, gain, shift):
    center = values - jnp.mean(values, -1, keepdims=True)
    spread = jnp.mean(center * center, -1, keepdims=True)
    return center * lax.rsqrt(spread + NORM_EPSILON) * gain + shift


def exact_gelu(values):
    return jax.nn.gelu(values, approximate=False)


def contract_rows(left, right):
    return lax.dot_general(
        left, right, (((0,), (0,)), ((), ())), preferred_element_type=jnp.float32
    )


def contract_cols(left, right):
    return lax.dot_general(
        left, right, (((1,), (1,)), ((), ())), preferred_element_type=jnp.float32
    )


def split_heads(block):
    return block.reshape(block.shape[0], 2, HD)


def pair_scores(query_part, key_part):
    factor = 1.0 / (RELAX_SCALE * math.sqrt(HD))
    return (
        jnp.einsum(
            "qhd,khd->hqk",
            split_heads(query_part),
            split_heads(key_part),
            preferred_element_type=jnp.float32,
        )
        * factor
    )


def kept_probs(scores, allowed, row_max, row_total):
    exp_terms = jnp.exp(jnp.where(allowed, RELAX_SCALE * (scores - row_max), -jnp.inf))
    return exp_terms / row_total


def body(
    tokens,
    cotangent,
    lengths,
    assign,
    w_qkv,
    qv_bias,
    w_out,
    out_bias,
    w_up,
    up_bias,
    w_down,
    down_bias,
    norm_gain,
    norm_shift,
):
    gathered = (
        lax.all_gather(w_qkv, ("seq", "dp"), axis=0, tiled=True),
        lax.all_gather(w_out, ("seq", "dp"), axis=0, tiled=True),
        lax.all_gather(w_up, ("seq", "dp"), axis=0, tiled=True),
        lax.all_gather(w_down, ("seq", "dp"), axis=0, tiled=True),
        lax.all_gather(qv_bias, ("seq", "dp"), axis=1, tiled=True),
        lax.all_gather(out_bias, ("seq", "dp"), axis=0, tiled=True),
        lax.all_gather(up_bias, ("seq", "dp"), axis=0, tiled=True),
        lax.all_gather(down_bias, ("seq", "dp"), axis=0, tiled=True),
        lax.all_gather(norm_gain, ("seq", "dp"), axis=1, tiled=True),
        lax.all_gather(norm_shift, ("seq", "dp"), axis=1, tiled=True),
    )
    qkv_full, out_full, up_full, down_full = (gathered[0], gathered[1], gathered[2], gathered[3])
    qv_shift = gathered[4].astype(jnp.float32)
    out_shift = gathered[5].astype(jnp.float32)
    up_shift = gathered[6].astype(jnp.float32)
    down_shift = gathered[7].astype(jnp.float32)
    gains = gathered[8].astype(jnp.float32)
    shifts = gathered[9].astype(jnp.float32)
    row_count = tokens.shape[1]
    model_width = tokens.shape[2]
    pair_cols = 2 * HD
    pair_count = model_width // pair_cols
    slot_rows = row_count * lax.axis_size("seq")
    factor = 1.0 / (RELAX_SCALE * math.sqrt(HD))
    valid = lengths[assign[lax.axis_index("dp")]]
    own_place = lax.axis_index("seq") * row_count + jnp.arange(row_count, dtype=jnp.int32)
    all_place = jnp.arange(slot_rows, dtype=jnp.int32)
    allowed = (all_place[None, :] <= own_place[:, None]) & (all_place[None, :] < valid)
    pair_ids = jnp.arange(pair_count, dtype=jnp.int32)
    hidden = tokens[0].astype(jnp.float32)
    normed_first, pull_first = jax.vjp(norm_rows, hidden, gains[0], shifts[0])
    normed_low = normed_first.astype(jnp.bfloat16)
    projected = jnp.dot(normed_low, qkv_full, preferred_element_type=jnp.float32)
    queries = (projected[:, :model_width] + qv_shift[0]).astype(jnp.bfloat16)
    key_own = projected[:, model_width : 2 * model_width].astype(jnp.bfloat16)
    value_own = (projected[:, 2 * model_width :] + qv_shift[1]).astype(jnp.bfloat16)
    keys, values = (
        lax.all_gather(key_own, "seq", axis=0, tiled=True),
        lax.all_gather(value_own, "seq", axis=0, tiled=True),
    )

    def columns(block, pair_index):
        return lax.dynamic_slice_in_dim(block, pair_index * pair_cols, pair_cols, 1)

    def merge_pairs(stack):
        return stack.transpose(1, 0, 2).reshape(stack.shape[1], model_width)

    def attend(pair_index):
        scores = pair_scores(columns(queries, pair_index), columns(keys, pair_index))
        row_max = jnp.max(jnp.where(allowed, scores, -jnp.inf), -1, keepdims=True)
        exp_terms = jnp.exp(jnp.where(allowed, RELAX_SCALE * (scores - row_max), -jnp.inf))
        row_total = jnp.sum(exp_terms, -1, keepdims=True)
        probs = (exp_terms / row_total).astype(jnp.bfloat16)
        mixed = jnp.einsum(
            "hqk,khd->qhd",
            probs,
            split_heads(columns(values, pair_index)),
            preferred_element_type=jnp.float32,
        )
        return (mixed.reshape(row_count, pair_cols), row_max[..., 0], row_total[..., 0])

    mixed_pairs, max_pairs, total_pairs = lax.map(attend, pair_ids)
    attended = merge_pairs(mixed_pairs).astype(jnp.bfloat16)
    branch = jnp.dot(attended, out_full, preferred_element_type=jnp.float32) + out_shift
    normed_second, pull_second = jax.vjp(norm_rows, branch, gains[1], shifts[1])
    middle = hidden + normed_second
    normed_third, pull_third = jax.vjp(norm_rows, middle, gains[2], shifts[2])
    third_low = normed_third.astype(jnp.bfloat16)
    up_pre = jnp.dot(third_low, up_full, preferred_element_type=jnp.float32) + up_shift
    activated, pull_gelu = jax.vjp(exact_gelu, up_pre)
    active_low = activated.astype(jnp.bfloat16)
    down_pre = jnp.dot(active_low, down_full, preferred_element_type=jnp.float32) + down_shift
    normed_fourth, pull_fourth = jax.vjp(norm_rows, down_pre, gains[3], shifts[3])
    output = (middle + normed_fourth).astype(jnp.bfloat16)[None]
    again = (
        lax.all_gather(w_qkv, ("seq", "dp"), axis=0, tiled=True),
        lax.all_gather(w_out, ("seq", "dp"), axis=0, tiled=True),
        lax.all_gather(w_up, ("seq", "dp"), axis=0, tiled=True),
        lax.all_gather(w_down, ("seq", "dp"), axis=0, tiled=True),
    )
    qkv_back, out_back, up_back, down_back = (again[0], again[1], again[2], again[3])
    keep_rows = (own_place < valid).astype(jnp.float32)[:, None]
    grad_out = cotangent[0].astype(jnp.float32) * keep_rows
    grad_down, grad_gain_four, grad_shift_four = pull_fourth(grad_out)
    grad_down_low = grad_down.astype(jnp.bfloat16)
    grad_w_down = contract_rows(active_low, grad_down_low)
    grad_b_down = jnp.sum(grad_down_low.astype(jnp.float32), 0)
    (grad_up,) = pull_gelu(contract_cols(grad_down_low, down_back))
    grad_up_low = grad_up.astype(jnp.bfloat16)
    grad_w_up = contract_rows(third_low, grad_up_low)
    grad_b_up = jnp.sum(grad_up_low.astype(jnp.float32), 0)
    grad_middle_part, grad_gain_three, grad_shift_three = pull_third(
        contract_cols(grad_up_low, up_back)
    )
    grad_middle = grad_out + grad_middle_part
    grad_branch, grad_gain_two, grad_shift_two = pull_second(grad_middle)
    grad_branch_low = grad_branch.astype(jnp.bfloat16)
    grad_w_out = contract_rows(attended, grad_branch_low)
    grad_b_out = jnp.sum(grad_branch_low.astype(jnp.float32), 0)
    grad_attended = contract_cols(grad_branch_low, out_back).astype(jnp.bfloat16)

    def query_side(pair_index):
        scores = pair_scores(columns(queries, pair_index), columns(keys, pair_index))
        probs = kept_probs(
            scores, allowed, max_pairs[pair_index][..., None], total_pairs[pair_index][..., None]
        )
        grad_part = columns(grad_attended, pair_index)
        grad_probs = jnp.einsum(
            "qhd,khd->hqk",
            split_heads(grad_part),
            split_heads(columns(values, pair_index)),
            preferred_element_type=jnp.float32,
        )
        delta = jnp.sum(probs * grad_probs, -1, keepdims=True)
        grad_scores = (RELAX_SCALE * probs * (grad_probs - delta)).astype(jnp.bfloat16)
        grad_query = (
            jnp.einsum(
                "hqk,khd->qhd",
                grad_scores,
                split_heads(columns(keys, pair_index)),
                preferred_element_type=jnp.float32,
            )
            * factor
        )
        return (grad_query.reshape(row_count, pair_cols), grad_scores, probs, delta)

    def both_sides(pair_index):
        grad_query, grad_scores, probs, delta = query_side(pair_index)
        grad_part = columns(grad_attended, pair_index)
        grad_key = (
            jnp.einsum(
                "hqk,qhd->khd",
                grad_scores,
                split_heads(columns(queries, pair_index)),
                preferred_element_type=jnp.float32,
            )
            * factor
        )
        grad_value = jnp.einsum(
            "hqk,qhd->khd",
            probs.astype(jnp.bfloat16),
            split_heads(grad_part),
            preferred_element_type=jnp.float32,
        )
        return (
            grad_query,
            grad_key.reshape(slot_rows, pair_cols),
            grad_value.reshape(slot_rows, pair_cols),
        )

    query_pairs, key_terms, value_terms = lax.map(both_sides, pair_ids)
    key_pairs, value_pairs = (
        lax.psum_scatter(
            key_terms.astype(jnp.bfloat16), "seq", scatter_dimension=1, tiled=True
        ).astype(jnp.float32),
        lax.psum_scatter(
            value_terms.astype(jnp.bfloat16), "seq", scatter_dimension=1, tiled=True
        ).astype(jnp.float32),
    )
    grad_q_low = merge_pairs(query_pairs).astype(jnp.bfloat16)
    grad_k_low = merge_pairs(key_pairs).astype(jnp.bfloat16)
    grad_v_low = merge_pairs(value_pairs).astype(jnp.bfloat16)
    grad_projected = jnp.concatenate([grad_q_low, grad_k_low, grad_v_low], 1)
    grad_w_qkv = contract_rows(normed_low, grad_projected)
    grad_qv = jnp.stack(
        [jnp.sum(grad_q_low.astype(jnp.float32), 0), jnp.sum(grad_v_low.astype(jnp.float32), 0)]
    )
    grad_hidden_part, grad_gain_one, grad_shift_one = pull_first(
        contract_cols(grad_projected, qkv_back)
    )
    input_grad = (grad_middle + grad_hidden_part).astype(jnp.bfloat16)[None]
    grad_gains = jnp.stack([grad_gain_one, grad_gain_two, grad_gain_three, grad_gain_four])
    grad_shifts = jnp.stack([grad_shift_one, grad_shift_two, grad_shift_three, grad_shift_four])
    owned = (
        lax.psum_scatter(grad_w_qkv, ("seq", "dp"), scatter_dimension=0, tiled=True),
        lax.psum_scatter(grad_w_out, ("seq", "dp"), scatter_dimension=0, tiled=True),
        lax.psum_scatter(grad_w_up, ("seq", "dp"), scatter_dimension=0, tiled=True),
        lax.psum_scatter(grad_w_down, ("seq", "dp"), scatter_dimension=0, tiled=True),
        lax.psum_scatter(grad_qv, ("seq", "dp"), scatter_dimension=1, tiled=True),
        lax.psum_scatter(grad_b_out, ("seq", "dp"), scatter_dimension=0, tiled=True),
        lax.psum_scatter(grad_b_up, ("seq", "dp"), scatter_dimension=0, tiled=True),
        lax.psum_scatter(grad_b_down, ("seq", "dp"), scatter_dimension=0, tiled=True),
        lax.psum_scatter(grad_gains, ("seq", "dp"), scatter_dimension=1, tiled=True),
        lax.psum_scatter(grad_shifts, ("seq", "dp"), scatter_dimension=1, tiled=True),
    )
    return (
        output,
        input_grad,
        owned[0],
        owned[4],
        owned[1],
        owned[5],
        owned[2],
        owned[6],
        owned[3],
        owned[7],
        owned[8],
        owned[9],
    )


MESH = pl.DeviceIdType.MESH


def is_small(mesh):
    return mesh.shape["seq"] == 16 and mesh.shape["dp"] == 2


def place():
    seq = lax.axis_index("seq")
    return seq // 8, (seq // 4) % 2, (seq // 2) % 2, seq % 2, lax.axis_index("dp")


def exchange_copies(scatter, src, out, send_sem, recv_sem, own_sem):
    a, b, y, c, x = place()

    def peer(k):
        return lax.rem(a + k // 2, 2), lax.rem(y + k % 2, 2)

    def device(k):
        pa, py = peer(k)
        return (pa * 8 + b * 4 + py * 2 + c, x)

    def source(k):
        pa, py = peer(k)
        return src.at[pa * 2 + py] if scatter else src.at[pa, :, py]

    def target(k):
        pa, py = peer(k)
        return out.at[pa, :, py] if scatter else out.at[pa * 2 + py]

    def copy(k, dst):
        return pltpu.make_async_remote_copy(
            src_ref=source(k), dst_ref=target(dst), send_sem=send_sem.at[k], recv_sem=recv_sem.at[k],
            device_id=device(k), device_id_type=MESH)

    def greet():
        barrier = pltpu.get_barrier_semaphore()
        for k in range(1, 4):
            pl.semaphore_signal(barrier, inc=1, device_id=device(k), device_id_type=MESH)

    def run():
        own = pltpu.make_async_copy(source(0), target(0), own_sem)
        own.start()
        pl.semaphore_wait(pltpu.get_barrier_semaphore(), 3)
        for k in (3, 2, 1):
            copy(k, 0).start()
        own.wait()
        for k in (3, 2, 1):
            copy(k, k).wait_recv()
        for k in (3, 2, 1):
            copy(k, 0).wait_send()

    return greet, run


def row_block(i, j):
    _, b, _, c, _ = place()
    return pl.ds(pl.multiple_of(lax.rem(b + i, 2) * 256 + lax.rem(c + j, 2) * 128, 128), 128)


def to_heads_kernel(rows_ref, out, src, *sems):
    greet, run = exchange_copies(True, src, out, *sems)
    greet()
    low = src.shape[2] - 128
    for g in range(4):
        values = slice(low * 2 + g * HD, low * 2 + g * HD + HD)
        for i in range(2):
            if low:
                for j in range(2):
                    src[g, i, j * 128:j * 128 + 128] = rows_ref[row_block(i, j), g * 128:g * 128 + 128]
            src[g, i, low:] = jnp.concatenate([rows_ref[row_block(i, j), values] for j in range(2)], 1)
    run()


def from_heads_kernel(heads_ref, out, got, *sems):
    greet, run = exchange_copies(False, heads_ref, got, *sems)
    greet()
    run()
    low = got.shape[2] - 128
    c = place()[3]
    for i in range(2):
        if low:
            for j in range(2):
                for g in range(4):
                    out[row_block(i, j), g * 128:g * 128 + 128] = got[g, i, j * 128:j * 128 + 128]
        for g in (0, 2):
            left, right = got[g, i, low:], got[g + 1, i, low:]
            cols = slice(low * 2 + g * HD, low * 2 + g * HD + 128)
            for j in range(2):
                lanes = slice(j * HD, j * HD + HD)
                out[row_block(i, j), cols] = jnp.concatenate([left[:, lanes], right[:, lanes]], 1)


def exchange(blocks, scatter, cid):
    vm = pl.BlockSpec(memory_space=pltpu.VMEM)
    rows = blocks.shape[-1] // 2 if scatter else blocks.shape[-2]
    shape, held = (2, 2, 2, rows, 128), (4, 2, rows, 128)
    return pl.pallas_call(
        to_heads_kernel if scatter else from_heads_kernel,
        out_shape=jax.ShapeDtypeStruct(shape if scatter else (512, rows * 2), blocks.dtype),
        in_specs=[vm], out_specs=vm,
        scratch_shapes=[pltpu.VMEM(held, blocks.dtype), pltpu.SemaphoreType.DMA((4,)), pltpu.SemaphoreType.DMA((4,)),
                        pltpu.SemaphoreType.DMA],
        compiler_params=pltpu.CompilerParams(collective_id=cid, has_side_effects=True),
        cost_estimate=pl.CostEstimate(flops=0, bytes_accessed=rows * 100000, transcendentals=0),
        name="to_heads" if scatter else "from_heads",
    )(blocks)


def dot_nt(a, b):
    return lax.dot_general(a, b, (((1,), (1,)), ((), ())), preferred_element_type=jnp.float32)


def dot_nn(a, b):
    return jnp.dot(a, b, preferred_element_type=jnp.float32)


BQ = 256
MASKED = -1e30


def load_heads(valid, packed, q_ref, k_ref):
    rows = q_ref.shape[0]
    qk = packed[:, :256].reshape(rows, 128)
    kq = jnp.concatenate([qk[:, 64:], qk[:, :64]], axis=1)
    lane = lax.broadcasted_iota(jnp.int32, (rows, 128), 1)
    spot = lax.broadcasted_iota(jnp.int32, (rows, 128), 0)
    past = jnp.where(spot < valid, 0.0, MASKED)
    q_ref[...] = jnp.where(lane < 64, qk.astype(jnp.float32), jnp.where(lane == 64, 1.0, 0.0)).astype(jnp.bfloat16)
    k_ref[...] = jnp.where(lane < 64, kq.astype(jnp.float32), jnp.where(lane == 64, past, 0.0)).astype(jnp.bfloat16)


def unpack_rows(halves):
    n = halves.shape[0]
    return jnp.concatenate([halves[:, :, :64], halves[:, :, 64:]], axis=1).reshape(n * 256, 64)


def block_probs(q_ref, k_ref, i):
    n = (i + 1) * BQ
    scores = dot_nt(k_ref[:n], q_ref[i * BQ:n])
    key = lax.broadcasted_iota(jnp.int32, (BQ, BQ), 0)
    query = lax.broadcasted_iota(jnp.int32, (BQ, BQ), 1)
    corner = jnp.where(key <= query, scores[n - BQ:], MASKED)
    scores = jnp.concatenate([scores[:n - BQ], corner], axis=0) if i else corner
    top = jnp.max(scores, axis=0, keepdims=True)
    terms = jnp.exp((scores - top) * 0.125)
    return terms, 1.0 / jnp.sum(terms, axis=0, keepdims=True)


def attend_kernel(valid_ref, packed, out_ref, q_ref, k_ref, vt_ref):
    load_heads(valid_ref[0], packed, q_ref, k_ref)
    unit = jnp.where(
        lax.broadcasted_iota(jnp.int32, (64, 64), 0) == lax.broadcasted_iota(jnp.int32, (64, 64), 1), 1.0, 0.0
    ).astype(jnp.bfloat16)
    vt_ref[...] = dot_nt(unit, unpack_rows(packed[:, 256:])).astype(jnp.bfloat16)
    for i in range(q_ref.shape[0] // BQ):
        n = (i + 1) * BQ
        terms, scale = block_probs(q_ref, k_ref, i)
        probs = (terms * scale).astype(jnp.bfloat16)
        mixed = dot_nn(vt_ref[:, :n], probs).T
        out_ref[i] = jnp.concatenate([mixed[:128], mixed[128:]], axis=1).astype(jnp.bfloat16)


def attend_back_kernel(valid_ref, packed, grad, out_ref, q_ref, k_ref, v_ref, g_ref, kt_ref, dk_ref, dv_ref):
    load_heads(valid_ref[0], packed, q_ref, k_ref)
    v_ref[...] = unpack_rows(packed[:, 256:])
    g_ref[...] = unpack_rows(grad[...])
    unit = jnp.where(
        lax.broadcasted_iota(jnp.int32, (64, 128), 0) == lax.broadcasted_iota(jnp.int32, (64, 128), 1), 1.0, 0.0
    ).astype(jnp.bfloat16)
    kt_ref[...] = dot_nt(unit, k_ref[...]).astype(jnp.bfloat16)
    dk_ref[...] = jnp.zeros_like(dk_ref)
    dv_ref[...] = jnp.zeros_like(dv_ref)
    blocks = q_ref.shape[0] // BQ
    for i in range(blocks):
        n = (i + 1) * BQ
        terms, scale = block_probs(q_ref, k_ref, i)
        probs = terms * scale
        grad_probs = dot_nt(v_ref[:n], g_ref[i * BQ:n])
        delta = jnp.sum(probs * grad_probs, axis=0, keepdims=True)
        grad_scores = (probs * (grad_probs - delta)).astype(jnp.bfloat16)
        grad_query = dot_nn(kt_ref[:, :n], grad_scores).T * 0.125
        out_ref[i, :256, :64] = grad_query.astype(jnp.bfloat16)
        dk_ref[:n] += dot_nn(grad_scores, q_ref[i * BQ:n])
        dv_ref[:n] += dot_nn(probs.astype(jnp.bfloat16), g_ref[i * BQ:n])
    for i in range(blocks):
        rows = slice(i * BQ, (i + 1) * BQ)
        out_ref[i, :256, 64:] = (dk_ref[rows, :64] * 0.125).astype(jnp.bfloat16)
        value = dv_ref[rows].astype(jnp.bfloat16)
        out_ref[i, 256:] = jnp.concatenate([value[:128], value[128:]], axis=1)


def attend(valid, packed):
    rows = packed.shape[0] * 256
    vm = pl.BlockSpec(memory_space=pltpu.VMEM)
    return pl.pallas_call(
        attend_kernel,
        out_shape=jax.ShapeDtypeStruct((packed.shape[0], 128, 128), jnp.bfloat16),
        in_specs=[pl.BlockSpec(memory_space=pltpu.SMEM), vm], out_specs=vm,
        scratch_shapes=[pltpu.VMEM((rows, 128), jnp.bfloat16)] * 2 + [pltpu.VMEM((64, rows), jnp.bfloat16)],
        compiler_params=pltpu.CompilerParams(vmem_limit_bytes=48 << 20),
        name="attend",
    )(valid, packed)


def attend_back(valid, packed, grad):
    rows = packed.shape[0] * 256
    vm = pl.BlockSpec(memory_space=pltpu.VMEM)
    return pl.pallas_call(
        attend_back_kernel,
        out_shape=jax.ShapeDtypeStruct(packed.shape, jnp.bfloat16),
        in_specs=[pl.BlockSpec(memory_space=pltpu.SMEM), vm, vm], out_specs=vm,
        scratch_shapes=[pltpu.VMEM((rows, 128), jnp.bfloat16)] * 2 + [pltpu.VMEM((rows, 64), jnp.bfloat16)] * 2
        + [pltpu.VMEM((64, rows), jnp.bfloat16), pltpu.VMEM((rows, 128), jnp.float32), pltpu.VMEM((rows, 64), jnp.float32)],
        compiler_params=pltpu.CompilerParams(vmem_limit_bytes=48 << 20),
        name="attend_back",
    )(valid, packed, grad)


def flip(bits, block):
    return lax.ppermute(block, "seq", [(s, s ^ bits) for s in range(16)])


flip_a, flip_y = (functools.partial(flip, bits) for bits in (8, 2))


def flip_x(block):
    return lax.ppermute(block, "dp", [(0, 1), (1, 0)])


def after(value, *others):
    return lax.optimization_barrier((value,) + others)[0]


def pick(block, index, axis, keepdims=False):
    return lax.dynamic_index_in_dim(block, index, axis, keepdims=keepdims)


def cube_one(flip_one, block):
    return jnp.concatenate([block, flip_one(block)], 0)


def arrange_kernel(spot_ref, kept, *refs):
    out = refs[-1]
    i = pl.program_id(0)
    wide = len(out.shape) == 7

    @pl.when(i < 4)
    def _():
        if wide:
            for j in range(2):
                for k in range(2):
                    out[0, j, 0, k, 0] = kept[0, j, k]
        else:
            out[0, 0, 0] = kept[0]

    @pl.when(i >= 4)
    def _():
        if wide:
            for j in range(2):
                for k in range(2):
                    out[0, j, 0, k, 0] = refs[j][0, k]
        else:
            out[0, 0, 0] = refs[0][0]


def arrange(spot, kept, *received):
    def coords(i, r):
        return lax.rem(r[0] + i % 2, 2), lax.rem(r[1] + i // 4, 2), lax.rem(r[2] + (i // 2) % 2, 2)

    shape = kept.shape

    def spec(block, low):
        rest = (0,) * (block.ndim - 1)
        return pl.BlockSpec((1,) + block.shape[1:], lambda i, r: (jnp.clip(i - low, 0, 3),) + rest)

    if len(shape) == 5:
        def out_place(i, r):
            a, y, x = coords(i, r)
            return a, 0, y, 0, x, 0, 0
        out_block, out_shape = (1, 2, 1, 2, 1) + shape[3:], (2,) * 5 + shape[3:]
    else:
        def out_place(i, r):
            return coords(i, r) + (0, 0)
        out_block, out_shape = (1, 1, 1) + shape[1:], (2, 2, 2) + shape[1:]
    return pl.pallas_call(
        arrange_kernel,
        out_shape=jax.ShapeDtypeStruct(out_shape, kept.dtype),
        grid_spec=pltpu.PrefetchScalarGridSpec(
            num_scalar_prefetch=1, grid=(8,), in_specs=[spec(kept, 0)] + [spec(block, 4) for block in received],
            out_specs=pl.BlockSpec(out_block, out_place)),
        compiler_params=pltpu.CompilerParams(vmem_limit_bytes=32 << 20),
        cost_estimate=pl.CostEstimate(flops=0, bytes_accessed=8 << 20, transcendentals=0),
        name="arrange",
    )(spot, kept, *received)


def up_kernel(rows_ref, w_ref, shift_ref, active_ref, slope_ref):
    for r in range(0, rows_ref.shape[0], 128):
        span = slice(r, r + 128)
        t = dot_nn(rows_ref[span], w_ref[...]) + shift_ref[...]
        half = 0.5 + 0.5 * lax.erf(t * math.sqrt(0.5))
        active_ref[span] = (t * half).astype(jnp.bfloat16)
        slope_ref[span] = half + t * jnp.exp(t * t * -0.5) * (1.0 / math.sqrt(2.0 * math.pi))


def up_gelu(rows, w, shift):
    m, k = rows.shape
    n, block = w.shape[1], 256
    return pl.pallas_call(
        up_kernel, grid=(n // block,),
        out_shape=(jax.ShapeDtypeStruct((m, n), jnp.bfloat16), jax.ShapeDtypeStruct((m, n), jnp.float32)),
        in_specs=[pl.BlockSpec((m, k), lambda i: (0, 0)), pl.BlockSpec((k, block), lambda i: (0, i)),
                  pl.BlockSpec((1, block), lambda i: (0, i))],
        out_specs=(pl.BlockSpec((m, block), lambda i: (0, i)),) * 2,
        compiler_params=pltpu.CompilerParams(vmem_limit_bytes=32 << 20),
        cost_estimate=pl.CostEstimate(flops=2 * m * n * k, bytes_accessed=24 << 20, transcendentals=2 * m * n),
        name="up_gelu",
    )(rows, w, shift)


def add_low(mine, other):
    return (mine.astype(jnp.float32) + other.astype(jnp.float32)).astype(jnp.bfloat16)


def fold(terms, flip_one, index, axis):
    return add_low(pick(terms, index, axis, True), flip_one(pick(terms, 1 - index, axis, True)))


def reduce_kernel(q_ref, o_ref, u_ref, part, tokens, grad_middle, vectors, *refs):
    vec_refs, (out_q, ro, out_u, vec, input_grad, got_far, got_near, low_sums, got_sums, row_send, row_recv, rq, gu, r1q, t2q, r2q, t3q, r3q, fq, gq, r1o, t2o, r2o, t3o, r3o,
               run, got, send_sem, recv_sem) = refs[:10], refs[10:]
    a, b, y, c, x = place()
    f32, bf16 = jnp.float32, jnp.bfloat16
    barrier = pltpu.get_barrier_semaphore()

    def at(pa, pb, py, pc, px):
        return (pa * 8 + pb * 4 + py * 2 + pc, px)

    to_x, to_y, to_a = at(a, b, y, c, 1 - x), at(a, b, 1 - y, c, x), at(1 - a, b, y, c, x)
    ranks = [(lax.rem(b + k // 2, 2), lax.rem(c + k % 2, 2)) for k in range(4)]
    to_rank = [at(a, ranks[k][0], y, ranks[k][1], x) for k in range(4)]
    to_b, to_c = to_rank[2], to_rank[1]
    for dev in [to_x, to_y, to_a] + to_rank[1:]:
        pl.semaphore_signal(barrier, inc=1, device_id=dev, device_id_type=MESH)
    for pb in range(2):
        for j in range(4):
            for row, cols in ((0, slice(j * 128, j * 128 + HD)), (1, slice(512 + j * HD, 512 + j * HD + HD))):
                piece = vec_refs[0][:, cols]
                pair = [jnp.where((b == pb) & (c == pc), piece, 0.0) for pc in range(2)]
                h = head_of(j // 2, pb, j % 2, 0) * HD
                run[0, row:row + 1, h:h + 128] = jnp.concatenate(pair, 1)
            for pc in range(2):
                col = head_of(j // 2, pb, j % 2, pc) * 256
                piece = vec_refs[1][:, j * 256:j * 256 + 256]
                run[0, 12 + col // 1024:13 + col // 1024, col % 1024:col % 1024 + 256] = jnp.where(
                    (b == pb) & (c == pc), piece, 0.0)
    for k, row in enumerate((2, 3, 5, 6, 7, 9, 10, 11)):
        run[0, row:row + 1] = vec_refs[2 + k][...]
    for row in (4, 8):
        run[0, row:row + 1] = jnp.zeros((1, 1024), f32)
    pl.semaphore_wait(barrier, 6)

    made = []

    def remote(src, dst, dev):
        k = len(made)
        made.append(pltpu.make_async_remote_copy(
            src_ref=src, dst_ref=dst, send_sem=send_sem.at[k], recv_sem=recv_sem.at[k],
            device_id=dev, device_id_type=MESH))
        return made[-1]

    def low(*values):
        return sum(v.astype(f32) for v in values)

    places = [1 - a, a]
    halves = [slice(0, 512), slice(512, 1024)]
    lateral = [(to_x, to_y), (to_y, to_x)]

    q1, q2, o1, o2 = {}, {}, {}, {}
    for i in range(2):
        for s in range(2):
            p = places[i]
            q1[s, i] = remote(q_ref.at[p, 0, :, :, 1 - x] if s == 0 else q_ref.at[p, 1, 1 - y], r1q.at[s, i], lateral[s][0])
            o1[s, i] = remote(o_ref.at[p, :, 1 - x, :, halves[0]] if s == 0 else o_ref.at[p, 1 - y, :, :, halves[1]],
                              r1o.at[s, i], lateral[s][0])
            q2[s, i] = remote(t2q.at[s, i], r2q.at[s, i], lateral[s][1])
            o2[s, i] = remote(t2o.at[s, i], r2o.at[s, i], lateral[s][1])
    q3 = [remote(t3q.at[s], r3q.at[s], to_a) for s in range(2)]
    o3 = [remote(t3o.at[s], r3o.at[s], to_a) for s in range(2)]
    qr = [remote(fq.at[ranks[k][0], ranks[k][1]], gq.at[k - 1], to_rank[k]) for k in range(1, 4)]
    ur = [remote(u_ref.at[ranks[k][0], ranks[k][1]], gu.at[b, c], to_rank[k]) for k in range(1, 4)]
    vs = [remote(run.at[k], got.at[k], dev) for k, dev in enumerate((to_x, to_y, to_a, to_b, to_c))]

    def next_sum(k):
        vs[k].wait_recv()
        if k < 4:
            run[k + 1] = run[k] + got[k]
            vs[k + 1].start()
        else:
            vec[...] = run[k] + got[k]

    pieces = part.shape[2] // PIECE

    def span(r):
        return pl.ds(pl.multiple_of(r * PIECE, PIECE), PIECE)

    def row_copy(kind, r):
        src, dst, dev = ((part.at[1, 1, span(r)], got_far.at[span(r)], to_c), (part.at[0, 1, span(r)], got_near.at[span(r)], to_c),
                         (low_sums.at[span(r)], got_sums.at[span(r)], to_b))[kind]
        return pltpu.make_async_remote_copy(
            src_ref=src, dst_ref=dst, send_sem=row_send.at[kind, r], recv_sem=row_recv.at[kind, r],
            device_id=dev, device_id_type=MESH)

    def send_across(r, _):
        row_copy(0, r).wait_recv()
        low_sums[span(r)] = (part[1, 0, span(r)] + got_far[span(r)]).astype(bf16)
        row_copy(2, r).start()
        return 0

    def take(r, _):
        row_copy(1, r).wait_recv()
        row_copy(2, r).wait_recv()
        total = part[0, 0, span(r)] + got_near[span(r)] + got_sums[span(r)].astype(f32)
        _, pull = jax.vjp(norm_rows, tokens[span(r)].astype(f32), *norm_vectors(vectors, 0))
        term, grad_gain, grad_shift = pull(total)
        input_grad[span(r)] = (grad_middle[span(r)] + term).astype(bf16)
        run[0, 4:5] += grad_gain
        run[0, 8:9] += grad_shift
        for kind in range(3):
            row_copy(kind, r).wait_send()
        return 0

    for kind in range(2):
        for r in range(pieces):
            row_copy(kind, r).start()
    for s in range(2):
        q1[s, 0].start()
        o1[s, 0].start()
    for k in (3, 2, 1):
        ur[k - 1].start()
    for s in range(2):
        o1[s, 1].start()
    lax.fori_loop(0, pieces, send_across, 0)

    def q_terms(s, i, far):
        p = places[i]
        if s == 0:
            v = 1 - y if far else y
            return q_ref[p, 0, v, :, x], r1q[0, i, v]
        v = 1 - x if far else x
        return q_ref[p, 1, y, :, v], r1q[1, i, :, v]

    def o_terms(s, i, far):
        p = places[i]
        if s == 0:
            v = 1 - y if far else y
            return o_ref[p, v, x, :, halves[0]], r1o[0, i, v]
        v = 1 - x if far else x
        return o_ref[p, y, v, :, halves[1]], r1o[1, i, v]

    for i in range(2):
        for s in range(2):
            q1[s, i].wait_recv()
            t2q[s, i] = low(*q_terms(s, i, True)).astype(bf16)
            q2[s, i].start()
            o1[s, i].wait_recv()
            t2o[s, i] = low(*o_terms(s, i, True)).astype(bf16)
            o2[s, i].start()
        if i == 0:
            for s in range(2):
                q1[s, 1].start()
            lax.fori_loop(0, pieces, take, 0)
            vs[0].start()
            for s in range(2):
                q2[s, 0].wait_recv()
                t3q[s] = low(*q_terms(s, 0, False), r2q[s, 0]).astype(bf16)
                q3[s].start()
                o2[s, 0].wait_recv()
                t3o[s] = low(*o_terms(s, 0, False), r2o[s, 0]).astype(bf16)
                o3[s].start()
    next_sum(0)
    for s in range(2):
        q2[s, 1].wait_recv()
        o2[s, 1].wait_recv()
        q3[s].wait_recv()
        total = low(*q_terms(s, 1, False), r2q[s, 1], r3q[s])
        fq[s] = total.astype(bf16)
        for j in range(2):
            @pl.when((b == s) & (c == j))
            def _():
                rq[s, j] = total[j]
        o3[s].wait_recv()
        ro[:, halves[s]] = low(*o_terms(s, 1, False), r2o[s, 1], r3o[s])
        next_sum(1 + s)
    for k in (3, 2, 1):
        qr[k - 1].start()
    gu[b, c] = u_ref[b, c]
    for k in (1, 2, 3):
        ur[k - 1].wait_recv()
    next_sum(3)
    for k in (1, 2, 3):
        pb, pc = ranks[k]
        qr[k - 1].wait_recv()
        rq[pb, pc] = gq[k - 1].astype(f32)
    for pb in range(2):
        for j in range(4):
            zero, one = rq[pb, 0], rq[pb, 1]
            h = head_of(j // 2, pb, j % 2, 0) * HD
            q, k = slice(j * 128, j * 128 + HD), slice(j * 128 + HD, j * 128 + 128)
            v = slice(512 + j * HD, 512 + j * HD + HD)
            for t, cols in enumerate((q, k, v)):
                out_q[:, t * 1024 + h:t * 1024 + h + 128] = jnp.concatenate([zero[:, cols], one[:, cols]], 1)
            for pc in range(2):
                col = head_of(j // 2, pb, j % 2, pc) * 256
                out_u[:, col:col + 256] = gu[pb, pc, :, j * 256:j * 256 + 256].astype(f32)
    next_sum(4)
    for copy in made:
        copy.wait_send()


def reduce_all(gw_qkv, gw_out, up_sum, part, tokens, grad_middle, params, vectors, cid):
    f32, bf16 = jnp.float32, jnp.bfloat16
    V = pltpu.VMEM
    vm = pl.BlockSpec(memory_space=V)
    S = jax.ShapeDtypeStruct
    q, o, u = gw_qkv.shape[5:], (gw_out.shape[3], 512), up_sum.shape
    rows, n = grad_middle.shape
    scratch = [
        V((rows, n), f32), V((rows, n), f32), V((rows, n), bf16), V((rows, n), bf16),
        pltpu.SemaphoreType.DMA((3, rows // PIECE)), pltpu.SemaphoreType.DMA((3, rows // PIECE)),
        V((2, 2) + q, f32), V(u, bf16),
        V((2, 2, 2, 2) + q, bf16), V((2, 2, 2) + q, bf16), V((2, 2, 2) + q, bf16), V((2, 2) + q, bf16), V((2, 2) + q, bf16),
        V((2, 2) + q, bf16), V((3,) + q, bf16),
        V((2, 2, 2) + o, bf16), V((2, 2) + o, bf16), V((2, 2) + o, bf16), V((2,) + o, bf16), V((2,) + o, bf16),
        V((5, 16, 1024), f32), V((5, 16, 1024), f32),
        pltpu.SemaphoreType.DMA((32,)), pltpu.SemaphoreType.DMA((32,))]
    return pl.pallas_call(
        reduce_kernel,
        out_shape=(S((q[0], 4 * q[1]), f32), S((o[0], 1024), f32), S((u[2], 4 * u[3]), f32), S((16, 1024), f32), S((rows, n), bf16)),
        in_specs=[vm] * 17, out_specs=(vm,) * 5, scratch_shapes=scratch,
        compiler_params=pltpu.CompilerParams(collective_id=cid, has_side_effects=True, vmem_limit_bytes=48 << 20),
        name="reduce_all",
    )(gw_qkv, gw_out, up_sum, part.reshape(2, 2, rows, n), tokens, grad_middle, params, *vectors)


def qk_columns(head):
    return slice(head * HD, head * HD + HD), slice(1024 + head * HD, 1024 + head * HD + HD), slice(2048 + head * HD, 2048 + head * HD + HD)


def head_of(a, b, y, c):
    return a * 8 + b * 4 + y * 2 + c


def start_kernel(q_hbm, u_hbm, o_in, t_in, v_in, wq, wo, up, rows, vec, q_in, u_in, q_src, u_src, send_sem, recv_sem, own_sem):
    a, b, y, c, x = place()
    barrier = pltpu.get_barrier_semaphore()

    def at(pa, pb, py, pc, px):
        return (pa * 8 + pb * 4 + py * 2 + pc, px)

    to_x, to_y, to_a = at(a, b, y, c, 1 - x), at(a, b, 1 - y, c, x), at(1 - a, b, y, c, x)
    ranks = [(lax.rem(b + k // 2, 2), lax.rem(c + k % 2, 2)) for k in range(4)]
    to_rank = [at(a, pb, y, pc, x) for pb, pc in ranks]
    for dev in [to_x, to_y, to_a] + to_rank[1:]:
        pl.semaphore_signal(barrier, inc=1, device_id=dev, device_id_type=MESH)

    loads = [pltpu.make_async_copy(q_hbm, q_in, own_sem.at[5]), pltpu.make_async_copy(u_hbm, u_in, own_sem.at[6])]
    for copy in loads:
        copy.start()
    for copy in loads:
        copy.wait()

    for pb in range(2):
        for pc in range(2):
            for j in range(4):
                q, k, v = qk_columns(head_of(j // 2, pb, j % 2, pc))
                q_src[pb, pc, :, j * 128:j * 128 + 128] = jnp.concatenate([q_in[:, q], q_in[:, k]], 1)
            for j in range(2):
                v0 = qk_columns(head_of(j, pb, 0, pc))[2]
                v1 = qk_columns(head_of(j, pb, 1, pc))[2]
                q_src[pb, pc, :, 512 + j * 128:640 + j * 128] = jnp.concatenate([q_in[:, v0], q_in[:, v1]], 1)
            for j in range(4):
                col = (head_of(j // 2, pb, j % 2, pc)) * 256
                u_src[pb, pc, :, j * 256:j * 256 + 256] = u_in[:, col:col + 256]
    own = [pltpu.make_async_copy(src, dst, own_sem.at[k]) for k, (src, dst) in enumerate((
        (q_src.at[b, c], wq.at[a, b, y, c, x]), (u_src.at[b, c], up.at[0, b, c]), (o_in, wo.at[a, y, x]),
        (t_in, rows.at[0]), (v_in, vec.at[a, b, y, c, x])))]
    for copy in own:
        copy.start()
    pl.semaphore_wait(barrier, 6)

    made = []

    def remote(src, dst, dev):
        k = len(made)
        made.append(pltpu.make_async_remote_copy(
            src_ref=src, dst_ref=dst, send_sem=send_sem.at[k], recv_sem=recv_sem.at[k],
            device_id=dev, device_id_type=MESH))
        return made[-1]

    places = [a, 1 - a]
    halves = [slice(0, 512), slice(512, 1024)]
    lateral = [(to_y, to_x), (to_x, to_y)]

    def same(ref, dev):
        return remote(ref, ref, dev)

    q_rank = [remote(q_src.at[ranks[k][0], ranks[k][1]], wq.at[a, b, y, c, x], to_rank[k]) for k in range(1, 4)]
    u_rank = [remote(u_src.at[ranks[k][0], ranks[k][1]], up.at[0, b, c], to_rank[k]) for k in range(1, 4)]
    v_rank = [remote(v_in, vec.at[a, b, y, c, x], to_rank[k]) for k in range(1, 4)]
    t_core, t_near = remote(t_in, rows.at[1], to_rank[1]), remote(t_in, rows.at[2], to_rank[2])
    t_far = remote(rows.at[2], rows.at[3], to_rank[1])
    u_cube = remote(up.at[0], up.at[1], to_a)
    v_cube = [same(vec.at[a, :, y, :, x], to_a), same(vec.at[:, :, y, :, x], to_y), same(vec.at[:, :, :, :, x], to_x)]
    q_cube = [same(wq.at[a, s, y, :, x], to_a) for s in range(2)]
    o_cube = [remote(o_in.at[:, halves[s]], wo.at[a, y, x, :, halves[s]], to_a) for s in range(2)]
    q_side, o_side = {}, {}
    for i in range(2):
        for s in range(2):
            one, two = lateral[s]
            oy, ox = (1 - y, x) if s == 0 else (y, 1 - x)
            p = places[i]
            mine, theirs = wq.at[p, s, y, :, x], wq.at[p, s, oy, :, ox]
            q_side[s, i] = (same(mine, one), same(mine, two), same(theirs, two))
            mine, theirs = wo.at[p, y, x, :, halves[s]], wo.at[p, oy, ox, :, halves[s]]
            first = o_in.at[:, halves[s]] if i == 0 else mine
            o_side[s, i] = (remote(first, mine, one), remote(first, mine, two), same(theirs, two))

    for k in (2, 1, 0):
        q_rank[k].start()
        v_rank[k].start()
    for s in range(2):
        o_cube[s].start()
        o_side[s, 0][0].start()
        o_side[s, 0][1].start()
    t_near.start()
    t_core.start()
    own[0].wait()
    for copy in q_rank:
        copy.wait_recv()
    for s in range(2):
        q_cube[s].start()
        q_side[s, 0][0].start()
        q_side[s, 0][1].start()
    own[4].wait()
    for copy in v_rank:
        copy.wait_recv()
    v_cube[0].start()
    for k in (2, 1, 0):
        u_rank[k].start()
    for s in range(2):
        o_side[s, 0][0].wait_recv()
        o_side[s, 0][2].start()
    for s in range(2):
        o_cube[s].wait_recv()
        o_side[s, 1][0].start()
        o_side[s, 1][1].start()
    t_near.wait_recv()
    t_far.start()
    for s in range(2):
        q_side[s, 0][0].wait_recv()
        q_side[s, 0][2].start()
    for s in range(2):
        q_cube[s].wait_recv()
        q_side[s, 1][0].start()
        q_side[s, 1][1].start()
    v_cube[0].wait_recv()
    v_cube[1].start()
    own[1].wait()
    for copy in u_rank:
        copy.wait_recv()
    u_cube.start()
    for s in range(2):
        o_side[s, 1][0].wait_recv()
        o_side[s, 1][2].start()
    v_cube[1].wait_recv()
    v_cube[2].start()
    for s in range(2):
        q_side[s, 1][0].wait_recv()
        q_side[s, 1][2].start()
    v_cube[2].wait_recv()
    t_core.wait_recv()
    t_far.wait_recv()
    for i in range(2):
        for s in range(2):
            for k in (1, 2):
                q_side[s, i][k].wait_recv()
                o_side[s, i][k].wait_recv()
    u_cube.wait_recv()
    for k in (2, 3):
        own[k].wait()
    for copy in made:
        copy.wait_send()


def start_gather(w_qkv, w_up, w_out, tokens, vectors, cid):
    bf16 = jnp.bfloat16
    S = lambda *shape: jax.ShapeDtypeStruct(shape, bf16)
    vm, anywhere = pl.BlockSpec(memory_space=pltpu.VMEM), pl.BlockSpec(memory_space=pl.ANY)
    return pl.pallas_call(
        start_kernel,
        out_shape=(S(2, 2, 2, 2, 2, 32, 768), S(2, 2, 2, 32, 1024), S(2, 2, 2, 32, 1024), S(4, 128, 1024),
                   S(2, 2, 2, 2, 2, 16, 128)),
        in_specs=[pl.BlockSpec(memory_space=pltpu.HBM)] * 4 + [vm], out_specs=(anywhere,) * 5,
        scratch_shapes=[
            pltpu.VMEM(w_qkv.shape, bf16), pltpu.VMEM(w_up.shape, bf16),
            pltpu.VMEM((2, 2, 32, 768), bf16), pltpu.VMEM((2, 2, 32, 1024), bf16),
            pltpu.SemaphoreType.DMA((48,)), pltpu.SemaphoreType.DMA((48,)), pltpu.SemaphoreType.DMA((7,))],
        compiler_params=pltpu.CompilerParams(collective_id=cid, has_side_effects=True, vmem_limit_bytes=63 << 20),
        cost_estimate=pl.CostEstimate(flops=0, bytes_accessed=100 << 20, transcendentals=0),
        name="start_gather",
    )(w_qkv, w_up, w_out, tokens, vectors)


PIECE = 32


def rows_kernel(step, gather, count_in, count_out, part, *refs):
    ins, outs = refs[:count_in], refs[count_in:count_in + count_out]
    rest = refs[count_in + count_out:]
    rows = rest[0] if gather else None
    got_far, got_near, sums, got_sums, send_sem, recv_sem = rest[-6:]
    a, b, y, c, x = place()

    def at(pb, pc):
        return (a * 8 + pb * 4 + y * 2 + pc, x)

    to_b, to_core = at(1 - b, c), at(b, 1 - c)
    barrier = pltpu.get_barrier_semaphore()
    for dev in (to_b, to_core):
        pl.semaphore_signal(barrier, inc=1, device_id=dev, device_id_type=MESH)
    pl.semaphore_wait(barrier, 2)
    pieces = part.shape[2] // PIECE

    def span(r):
        return pl.ds(pl.multiple_of(r * PIECE, PIECE), PIECE)

    def remote(kind, r, src, dst, dev):
        return pltpu.make_async_remote_copy(
            src_ref=src, dst_ref=dst, send_sem=send_sem.at[kind, r], recv_sem=recv_sem.at[kind, r],
            device_id=dev, device_id_type=MESH)

    def far(r):
        return remote(0, r, part.at[1, 1, span(r)], got_far.at[span(r)], to_core)

    def near(r):
        return remote(1, r, part.at[0, 1, span(r)], got_near.at[span(r)], to_core)

    def across(r):
        return remote(2, r, sums.at[span(r)], got_sums.at[span(r)], to_b)

    def row_near(r):
        return remote(3, r, rows.at[0, span(r)], rows.at[2, span(r)], to_b)

    def row_core(r):
        return remote(4, r, rows.at[0, span(r)], rows.at[1, span(r)], to_core)

    def row_far(r):
        return remote(5, r, rows.at[2, span(r)], rows.at[3, span(r)], to_core)

    for r in range(pieces):
        far(r).start()
    for r in range(pieces):
        near(r).start()

    def send_across(r, _):
        far(r).wait_recv()
        sums[span(r)] = (part[1, 0, span(r)] + got_far[span(r)]).astype(jnp.bfloat16)
        across(r).start()
        return 0

    lax.fori_loop(0, pieces, send_across, 0)
    for ref in outs:
        if ref.shape[0] == 1:
            ref[...] = jnp.zeros_like(ref)

    def take(r, _):
        near(r).wait_recv()
        across(r).wait_recv()
        total = part[0, 0, span(r)] + got_near[span(r)] + got_sums[span(r)].astype(jnp.float32)
        piece = step(span(r), total, ins, outs)
        if gather:
            rows[0, span(r)] = piece
            row_near(r).start()
            row_core(r).start()
        return 0

    lax.fori_loop(0, pieces, take, 0)

    def relay(r, _):
        row_near(r).wait_recv()
        row_far(r).start()
        return 0

    def finish(r, _):
        if gather:
            row_core(r).wait_recv()
            row_far(r).wait_recv()
            row_near(r).wait_send()
            row_core(r).wait_send()
            row_far(r).wait_send()
        far(r).wait_send()
        near(r).wait_send()
        across(r).wait_send()
        return 0

    if gather:
        lax.fori_loop(0, pieces, relay, 0)
    lax.fori_loop(0, pieces, finish, 0)


def sum_rows(step, part, ins, outs, gather, cid):
    rows, n = part.shape[0] // 4, part.shape[1]
    vm = pl.BlockSpec(memory_space=pltpu.VMEM)
    shapes = tuple(outs) + ((jax.ShapeDtypeStruct((4, rows, n), jnp.bfloat16),) if gather else ())
    V = pltpu.VMEM
    return pl.pallas_call(
        functools.partial(rows_kernel, step, gather, len(ins), len(outs)),
        out_shape=shapes, in_specs=[vm] * (1 + len(ins)), out_specs=(vm,) * len(shapes),
        scratch_shapes=[V((rows, n), jnp.float32), V((rows, n), jnp.float32), V((rows, n), jnp.bfloat16), V((rows, n), jnp.bfloat16),
                        pltpu.SemaphoreType.DMA((6, rows // PIECE)), pltpu.SemaphoreType.DMA((6, rows // PIECE))],
        compiler_params=pltpu.CompilerParams(collective_id=cid, has_side_effects=True, vmem_limit_bytes=32 << 20),
        cost_estimate=pl.CostEstimate(flops=0, bytes_accessed=50 << 20, transcendentals=0),
        name="sum_rows",
    )(part.reshape(2, 2, rows, n), *ins)


def norm_vectors(vectors, k):
    return vectors[4 + k:5 + k], vectors[8 + k:9 + k]


def attended_step(span, total, ins, outs):
    tokens, vectors = ins
    branch = total + vectors[2:3]
    middle = tokens[span].astype(jnp.float32) + norm_rows(branch, *norm_vectors(vectors, 1))
    outs[0][span] = branch
    outs[1][span] = middle
    return norm_rows(middle, *norm_vectors(vectors, 2)).astype(jnp.bfloat16)


def output_step(span, total, ins, outs):
    middle, grad_out, vectors = ins
    normed, pull = jax.vjp(norm_rows, total + vectors[3:4], *norm_vectors(vectors, 3))
    outs[0][span] = (middle[span] + normed).astype(jnp.bfloat16)
    grad_down, grad_gain, grad_shift = pull(grad_out[span])
    grad_down = grad_down.astype(jnp.bfloat16)
    outs[1][...] += grad_gain
    outs[2][...] += grad_shift
    outs[3][...] += jnp.sum(grad_down.astype(jnp.float32), 0, keepdims=True)
    return grad_down


def middle_step(span, total, ins, outs):
    middle, branch, grad_out, vectors = ins
    _, pull = jax.vjp(norm_rows, middle[span], *norm_vectors(vectors, 2))
    part, grad_gain2, grad_shift2 = pull(total)
    grad_middle = grad_out[span] + part
    _, pull = jax.vjp(norm_rows, branch[span], *norm_vectors(vectors, 1))
    grad_branch, grad_gain1, grad_shift1 = pull(grad_middle)
    grad_branch = grad_branch.astype(jnp.bfloat16)
    outs[0][span] = grad_middle
    for ref, value in zip(outs[1:], (grad_gain2, grad_shift2, grad_gain1, grad_shift1,
                                     jnp.sum(grad_branch.astype(jnp.float32), 0, keepdims=True))):
        ref[...] += value
    return grad_branch


def fast_body(tokens, cotangent, lengths, assign, w_qkv, qv_bias, w_out, out_bias, w_up, up_bias, w_down, down_bias,
              norm_gain, norm_shift):
    bf16, f32 = jnp.bfloat16, jnp.float32
    a, b, y, c, x = place()
    spot = jnp.stack([a, y, x]).astype(jnp.int32)
    width = tokens.shape[2]
    place_two = jnp.arange(2, dtype=jnp.int32)
    sequence = jnp.sum(jnp.where(place_two == x, assign.astype(jnp.int32), 0))
    valid = jnp.sum(jnp.where(place_two == sequence, lengths.astype(jnp.int32), 0))

    small, row = jnp.zeros((16, 128), bf16), 0
    for block in (qv_bias, out_bias[None], down_bias[None], norm_gain, norm_shift, up_bias[None]):
        small += jnp.pad(block, ((row, 16 - row - block.shape[0]), (0, 128 - block.shape[1])))
        row += block.shape[0]
    wqkv, wo, up_one, rows, small = start_gather(w_qkv, w_up, w_out, tokens[0], small, 6)
    down_one = after(w_down, wqkv)
    down_one = jnp.stack([down_one, flip_a(down_one)])
    wqkv, wo, rows = wqkv.reshape(width, 768), wo.reshape(256, width), rows.reshape(512, width)

    vectors = small[..., :12, :32].reshape(32, 12, 32).transpose(1, 0, 2).reshape(12, width).astype(f32)
    qv_half = pick(pick(vectors[:2].reshape(2, 2, 2, 2, 2, HD), b, 2), c, 3).reshape(2, 4, HD)
    qk_shift = jnp.concatenate([qv_half[0], jnp.zeros((4, HD), f32)], 1).reshape(512)
    v_shift = qv_half[1].reshape(256)
    up_shift = pick(pick(small[..., 12, :], b, 1), c, 2).reshape(1024).astype(f32)

    first = norm_rows(rows.astype(f32), vectors[4:5], vectors[8:9]).astype(bf16)
    up_two = cube_one(flip_x, up_one)
    projected = (dot_nn(first, wqkv) + jnp.concatenate([qk_shift, v_shift])).astype(bf16)
    packed = exchange(after(projected, up_two, down_one), True, 1).reshape(8, 384, 128)
    down_two = cube_one(flip_x, down_one)
    up_half = flip_y(after(up_two, packed)[:, 0])
    attended = attend(valid[None], packed).reshape(2, 2, 2, 128, 128)
    attended = exchange(after(attended, down_two, up_half), False, 2)
    up_rest = flip_y(after(up_two, attended)[:, 1])
    down_far = flip_y(after(down_two, attended))
    own_spot = lax.axis_index("seq") * 128 + jnp.arange(128, dtype=jnp.int32)
    grad_out = cotangent[0].astype(f32) * (own_spot < valid).astype(f32)[:, None]
    S = jax.ShapeDtypeStruct
    wide, low, line = S((128, width), f32), S((128, width), bf16), S((1, width), f32)
    branch, middle, third = sum_rows(
        attended_step, dot_nn(attended, wo), (tokens[0], vectors),
        (wide, wide), True, 7)
    third = third.reshape(512, width)
    wu = arrange(spot, up_two, up_half, up_rest).reshape(width, 1024)
    active, slope = up_gelu(third, wu, up_shift.reshape(1, 1024))
    wd = arrange(spot, down_two, after(down_far, active)).reshape(1024, width)
    output, gain4, shift4, bias_down, down_rows = sum_rows(
        output_step, dot_nn(active, wd), (middle, grad_out, vectors), (low, line, line, line), True, 8)
    down_rows = down_rows.reshape(512, width)
    gw_down = contract_rows(active, down_rows).astype(bf16).reshape(2, 2, 2, 128, width)
    down_term = flip_y(pick(gw_down, 1 - y, 1, True))
    grad_up = (dot_nt(after(down_rows, gw_down), wd) * slope).astype(bf16)
    gw_up = contract_rows(third, grad_up).astype(bf16).reshape(2, 2, 2, 2, 2, 32, 1024)
    up_term = flip_x(pick(gw_up, 1 - x, 4, True))
    grad_middle, gain3, shift3, gain2, shift2, bias_out, branch_rows = sum_rows(
        middle_step, after(dot_nt(grad_up, wu), gw_up),
        (middle, branch, grad_out, vectors), (wide,) + (line,) * 5, True, 9)
    branch_rows = branch_rows.reshape(512, width)
    grad_att = dot_nt(branch_rows, wo).astype(bf16)
    down_sum = add_low(pick(gw_down, y, 1, True), down_term)
    down_term = flip_x(pick(down_sum, 1 - x, 2, True))
    grad_packed = exchange(after(grad_att, down_sum), True, 3).reshape(8, 128, 128)
    up_sum = add_low(pick(gw_up, x, 4, True), after(up_term, grad_packed))
    up_term = flip_y(pick(up_sum, 1 - y, 2, True))
    down_sum = add_low(pick(down_sum, x, 2, True), after(down_term, grad_packed))
    down_term = flip_a(pick(down_sum, 1 - a, 0))
    back = attend_back(valid[None], packed, grad_packed)

    up_sum = add_low(pick(up_sum, y, 2, True), up_term)
    gw_out = contract_rows(attended, branch_rows).astype(bf16).reshape(2, 2, 2, 32, width)
    grad_qkv = exchange(after(back, up_sum, down_term).reshape(2, 2, 2, 384, 128), False, 4)
    up_term = flip_a(pick(after(up_sum, grad_qkv), 1 - a, 0))
    gw_qkv = contract_rows(first, grad_qkv).astype(bf16).reshape(2, 2, 2, 2, 2, 32, 768)
    def sums(block):
        return jnp.sum(block.astype(f32), 0, keepdims=True)

    sums_of = [sums(grad_qkv), sums(grad_up), bias_out, bias_down, gain2, gain3, gain4, shift2, shift3, shift4]
    up_sum = (pick(up_sum, a, 0).astype(f32) + up_term.astype(f32)).astype(bf16).reshape(2, 2, 32, 1024)
    r_qkv, r_out, r_up, vectors, input_grad = reduce_all(
        gw_qkv, gw_out, up_sum, dot_nt(grad_qkv, wqkv), tokens[0], grad_middle, vectors, sums_of, 5)
    r_down = (pick(down_sum, a, 0).astype(f32) + down_term.astype(f32)).reshape(128, width)
    index = lax.axis_index("seq") * 2 + x
    small_up = lax.dynamic_slice(vectors, (12 + index // 8, index % 8 * 128), (1, 128)).reshape(128)
    vectors = lax.dynamic_slice(vectors, (0, index * 32), (12, 32))

    return (
        output[None], input_grad[None], r_qkv, vectors[:2], r_out,
        vectors[2], r_up, small_up, r_down, vectors[3], vectors[4:8], vectors[8:12])


def solution(mesh):
    return jax.shard_map(
        fast_body if is_small(mesh) else body,
        mesh=mesh,
        in_specs=(
            P("dp", "seq", None),
            P("dp", "seq", None),
            P(),
            P(),
            P(("seq", "dp"), None),
            P(None, ("seq", "dp")),
            P(("seq", "dp"), None),
            P(("seq", "dp")),
            P(("seq", "dp"), None),
            P(("seq", "dp")),
            P(("seq", "dp"), None),
            P(("seq", "dp")),
            P(None, ("seq", "dp")),
            P(None, ("seq", "dp")),
        ),
        out_specs=(
            P("dp", "seq", None),
            P("dp", "seq", None),
            P(("seq", "dp"), None),
            P(None, ("seq", "dp")),
            P(("seq", "dp"), None),
            P(("seq", "dp")),
            P(("seq", "dp"), None),
            P(("seq", "dp")),
            P(("seq", "dp"), None),
            P(("seq", "dp")),
            P(None, ("seq", "dp")),
            P(None, ("seq", "dp")),
        ),
        check_vma=False,
    )
```

profile of v0, /device:TPU:0, one launch (start us, length us, event | category | flops | bytes accessed | tf_op | source)
XLA Modules:
  0.0 306.2 jit_solution(7640328656098882563)
XLA Ops:
  0.6 1.3 pad_add_fusion.v_in
  2.0 37.8 %start_gather.1 = (bf16[2,2,2,2,2,32,768]{6,5,4,3,2,1,0:T(8,128)(2,1)}, bf16[2,2,2,32,1024]{4,3,2,1,0:T(8,128)(2,1)}, bf16[2,2,2,32,1024]{4,3,2,1,0:T(8,128)(2,1...) custom-call(bf16[32,3072]{1,0:T(8,128)(2,1)} %q_hbm.1, bf16[32,4096]{1,0:T(8,128)(2,1)} %u_hbm.1, ...), custom_call_target="tpu_custom_call" | custom-call | bytes 104857600 | tf_op jit(solution)/shard_map/start_gather/pallas_call | solution.py:981
  41.2 1.6 collective-permute-start
  46.8 1.9 add_convert_fusion.3.rows_ref
  48.7 4.1 %collective-permute-done.1 = bf16[128,1024]{1,0:T(8,128)(2,1)S(1)} collective-permute-done((bf16[128,1024]{1,0:T(8,128)(2,1)}, bf16[128,1024]{1,0:T(8,128)(2,1)S(1)}, u32[]{:S(2)}, u32[]{:S(2)}) %collective-permute-start.1) | collective-permute-done | bytes 262176 | tf_op jit(solution)/shard_map/ppermute | solution.py:501
  53.6 1.5 collective-permute-start.2
  56.2 23.5 %to_heads.2 = bf16[2,2,2,384,128]{4,3,2,1,0:T(8,128)(2,1)} custom-call(bf16[512,768]{1,0:T(8,128)(2,1)} %add_convert_fusion.3.rows_ref), custom_call_target="tpu_custom_call" | custom-call | bytes 38400000 | tf_op jit(solution)/shard_map/to_heads/pallas_call | solution.py:378
  82.0 1.3 fusion.9
  84.4 8.0 %attend.1 = bf16[8,128,128]{2,1,0:T(8,128)(2,1)S(1)} custom-call(s32[1]{0:T(128)} %bitcast.valid_ref, bf16[8,384,128]{2,1,0:T(8,128)(2,1)S(1)} %bitcast.120), custom_call_target="tpu_custom_call" | custom-call | tf_op jit(solution)/shard_map/attend/pallas_call | solution.py:476
  94.4 10.9 %from_heads.2 = bf16[512,256]{1,0:T(8,128)(2,1)} custom-call(bf16[2,2,2,128,128]{4,3,2,1,0:T(8,128)(2,1)} %bitcast.136), custom_call_target="tpu_custom_call" | custom-call | bytes 12800000 | tf_op jit(solution)/shard_map/from_heads/pallas_call | solution.py:378
  110.7 16.1 %sum_rows.3 = (f32[128,1024]{1,0:T(8,128)S(1)}, f32[128,1024]{1,0:T(8,128)S(1)}, bf16[4,128,1024]{2,1,0:T(8,128)(2,1)S(1)}) custom-call(f32[2,2,128,1024]{3,2,1,0:T(8,128)S(1)} %fusion.15.part, bf16[128,1024]{1,0:T(8,128)(2,1)S(1)} %bitcast.124, f32[12,1024]{1,0:T(8,128)S(1)} %convert_element_type.173.refs_1_.refs_2_.refs_3_.vectors), custom_call_target="tpu_custom_call" | custom-call | bytes 52428800 | tf_op jit(solution)/shard_map/sum_rows/pallas_call | solution.py:1098
  127.7 14.1 %collective-permute-done.4.refs_1_ = bf16[4,2,32,1024]{3,2,1,0:T(8,128)(2,1)S(1)} collective-permute-done((bf16[4,2,32,1024]{3,2,1,0:T(8,128)(2,1)S(1)}, bf16[4,2,32,1024]{3,2,1,0:T(8,128)(2,1)S(1)}, u32[]{:S(2)}, u32[]{:S(2)}) %collective-permute-start.4) | collective-permute-done | bytes 524320 | tf_op jit(solution)/shard_map/ppermute | solution.py:501
  141.7 1.5 arrange.2
  143.2 3.1 %up_gelu.1 = (bf16[512,1024]{1,0:T(8,128)(2,1)S(1)}, f32[512,1024]{1,0:T(8,128)S(1)}) custom-call(bf16[512,1024]{1,0:T(8,128)(2,1)S(1)} %bitcast.140, bf16[1024,1024]{1,0:T(8,128)(2,1)S(1)} %bitcast.128, f32[1,1024]{1,0:T(1,128)S(1)} %convert.8.shift_ref), custom_call_target="tpu_custom_call" | custom-call | flops 1073741824 | bytes 25165824 | tf_op jit(solution)/shard_map/up_gelu/pallas_call | solution.py:590
  147.4 1.3 fusion.16.part
  148.6 16.0 %sum_rows.4 = (bf16[128,1024]{1,0:T(8,128)(2,1)S(1)}, f32[1,1024]{1,0:T(1,128)S(1)}, f32[1,1024]{1,0:T(1,128)S(1)}, f32[1,1024]{1,0:T(1,128)S(1)}, bf16[4,128,1024]{2,1,0:T(8,128)(2,1)S(1)}) custom-call(f32[2,2,128,1024]{3,2,1,0:T(8,128)S(1)} %fusion.16.part, f32[128,1024]{1,0:T(8,128)S(1)} %get-tuple-element.67.refs_0_, ...), custom_call_target="tpu_custom_call" | custom-call | bytes 52428800 | tf_op jit(solution)/shard_map/sum_rows/pallas_call | solution.py:1098
  164.7 1.3 convolution_convert_fusion.1
  168.3 1.3 convert_reduce_fusion
  169.6 1.3 convolution_convert_fusion
  173.8 1.5 fusion.3
  175.2 2.6 fusion.17
  177.8 16.7 %sum_rows.5 = (f32[128,1024]{1,0:T(8,128)S(1)}, f32[1,1024]{1,0:T(1,128)S(1)}, f32[1,1024]{1,0:T(1,128)S(1)}, f32[1,1024]{1,0:T(1,128)S(1)}, f32[1,1024]{1,0:T(1...) custom-call(f32[2,2,128,1024]{3,2,1,0:T(8,128)S(1)} %bitcast.127, ...), custom_call_target="tpu_custom_call" | custom-call | bytes 52428800 | tf_op jit(solution)/shard_map/sum_rows/pallas_call | solution.py:1098
  194.6 1.7 add_convert_fusion.1
  197.3 1.4 collective-permute-start.9
  199.9 11.1 %to_heads.3 = bf16[2,2,2,128,128]{4,3,2,1,0:T(8,128)(2,1)} custom-call(bf16[512,256]{1,0:T(8,128)(2,1)} %convolution_convert_fusion.4.rows_ref), custom_call_target="tpu_custom_call" | custom-call | bytes 12800000 | tf_op jit(solution)/shard_map/to_heads/pallas_call | solution.py:378
  211.0 1.7 add_convert_fusion
  215.8 11.6 %attend_back.1 = bf16[8,384,128]{2,1,0:T(8,128)(2,1)S(1)} custom-call(s32[1]{0:T(128)} %bitcast.valid_ref, bf16[8,384,128]{2,1,0:T(8,128)(2,1)S(1)} %bitcast.121, bf16[8,128,128]{2,1,0:T(8,128)(2,1)S(1)} %bitcast.135), custom_call_target="tpu_custom_call" | custom-call | tf_op jit(solution)/shard_map/attend_back/pallas_call | solution.py:489
  229.2 23.3 %from_heads.3 = bf16[512,768]{1,0:T(8,128)(2,1)} custom-call(bf16[2,2,2,384,128]{4,3,2,1,0:T(8,128)(2,1)} %bitcast.122), custom_call_target="tpu_custom_call" | custom-call | bytes 38400000 | tf_op jit(solution)/shard_map/from_heads/pallas_call | solution.py:378
  252.7 2.3 convolution_convert_fusion.2
  255.1 2.4 fusion.18.part
  258.5 7.2 %collective-permute-done.11 = bf16[2,1,2,1,32,1024]{5,4,2,0,3,1:T(8,128)(2,1)S(1)} collective-permute-done((bf16[2,1,2,1,32,1024]{5,4,2,0,3,1:T(8,128)(2,1)S(1)}, bf16[2,1,2,1,32,1024]{5,4,2,0,3,1:T(8,128)(2,1)S(1)}, u32[]{:S(2)}, u32[]{:S(2)}) %collective-permute-start.11) | collective-permute-done | bytes 262176 | tf_op jit(solution)/shard_map/ppermute | solution.py:501
  265.7 34.1 %reduce_all.1 = (f32[32,3072]{1,0:T(8,128)S(1)}, f32[32,1024]{1,0:T(8,128)S(1)}, f32[32,4096]{1,0:T(8,128)S(1)}, f32[16,1024]{1,0:T(8,128)S(1)}, bf16[128,1024]{1,0:T(8,128)(2,1)S(1)}) custom-call(bf16[2,2,2,2,2,32,768]{6,5,4,3,2,1,0:T(8,128)(2,1)S(1)} %bitcast.132, bf16[2,2,2,32,1024]{4,3,2,1,0:T(8,128)(2,1)S(1)} %bitcast.126, ...), custom_call_target="tpu_custom_call" | custom-call | tf_op jit(solution)/shard_map/reduce_all/pallas_call | solution.py:818
  (155 shorter events, 39.0 us)
Async XLA Ops:
  39.8 4.6 %copy-start.14 = (bf16[4,128,1024]{2,1,0:T(8,128)(2,1)S(1)}, bf16[4,128,1024]{2,1,0:T(8,128)(2,1)}, u32[]{:S(2)}) copy-start(bf16[4,128,1024]{2,1,0:T(8,128)(2,1)} %get-tuple-element.53) | copy-start | bytes 3145732
  39.8 13.0 %collective-permute-start.1 = (bf16[128,1024]{1,0:T(8,128)(2,1)}, bf16[128,1024]{1,0:T(8,128)(2,1)S(1)}, u32[]{:S(2)}, u32[]{:S(2)}) collective-permute-start(bf16[128,1024]{1,0:T(8,128)(2,1)} %param.24), channel_id=1, source_target_pairs={{0,16},{2,18},{4,20},{6,22},{8,24},{10,26},{12,28},{14,30},{16,0},... | collective-permute-start | bytes 786440 | tf_op jit(solution)/shard_map/ppermute | solution.py:501
  41.2 14.0 %collective-permute-start = (bf16[2,2,2,32,1024]{4,3,2,0,1:T(8,128)(2,1)S(1)}, bf16[2,2,2,32,1024]{4,3,2,0,1:T(8,128)(2,1)}, u32[]{:S(2)}, u32[]{:S(2)}) collective-permute-start(bf16[2,2,2,32,1024]{4,3,2,0,1:T(8,128)(2,1)S(1)} %get-tuple-element.96), channel_id=1, source_target_pairs={{0,1},{1,0},{2,3},{3,2},{4,5},{5,4},{6,7},{7,6},{8,9},{9,8},{10,11... | collective-permute-start | bytes 1572872 | tf_op jit(solution)/shard_map/ppermute | solution.py:508
  46.8 6.0 %copy-start.29 = (bf16[128,1024]{1,0:T(8,128)(2,1)S(1)}, bf16[128,1024]{1,0:T(8,128)(2,1)}, u32[]{:S(2)}) copy-start(bf16[128,1024]{1,0:T(8,128)(2,1)} %param.24) | copy-start | bytes 786436
  53.6 27.7 %copy-start.37 = (s32[2]{0:T(128)S(1)}, s32[2]{0:T(128)}, u32[]{:S(2)}) copy-start(s32[2]{0:T(128)} %param.17) | copy-start | bytes 28
  53.6 28.4 %copy-start.38 = (s32[2]{0:T(128)S(1)}, s32[2]{0:T(128)}, u32[]{:S(2)}) copy-start(s32[2]{0:T(128)} %param.16) | copy-start | bytes 28
  53.6 39.5 %collective-permute-start.2 = (bf16[2,128,1024]{2,1,0:T(8,128)(2,1)}, bf16[2,128,1024]{2,1,0:T(8,128)(2,1)}, u32[]{:S(2)}, u32[]{:S(2)}) collective-permute-start(bf16[2,128,1024]{2,1,0:T(8,128)(2,1)} %pad_maximum_fusion.1), channel_id=1, source_target_pairs={{0,1},{1,0},{2,3},{3,2},{4,5},{5,4},{6,7},{7,6},{8,9},{9,8},{10,11... | collective-permute-start | bytes 1572872 | tf_op jit(solution)/shard_map/ppermute | solution.py:508
  56.2 36.2 %copy-start.16 = (bf16[4,2,2,32,1024]{4,3,2,0,1:T(8,128)(2,1)}, bf16[4,2,2,32,1024]{4,3,2,0,1:T(8,128)(2,1)S(1)}, u32[]{:S(2)}) copy-start(bf16[4,2,2,32,1024]{4,3,2,0,1:T(8,128)(2,1)S(1)} %constant_dynamic-update-slice_fusion) | copy-start | bytes 3145732
  79.8 27.4 %copy-start.27 = (f32[32,12,32]{2,0,1:T(8,128)S(1)}, f32[32,12,32]{2,0,1:T(8,128)}, u32[]{:S(2)}) copy-start(f32[32,12,32]{2,0,1:T(8,128)} %copy-done.26) | copy-start | bytes 147460
  79.8 14.5 %collective-permute-start.3 = (bf16[4,2,32,1024]{3,2,1,0:T(8,128)(2,1)S(1)}, bf16[4,2,32,1024]{3,2,1,0:T(8,128)(2,1)S(1)}, u32[]{:S(2)}, u32[]{:S(2)}) collective-permute-start(bf16[4,2,32,1024]{3,2,1,0:T(8,128)(2,1)S(1)} %slice_bitcast_fusion.1), channel_id=1, source_target_pairs={{0,4},{2,6},{4,0},{6,2},{8,12},{10,14},{12,8},{14,10},{16,20},{18,... | collective-permute-start | bytes 1572872 | tf_op jit(solution)/shard_map/ppermute | solution.py:501
  93.2 16.5 %copy-start.32 = (bf16[1,128,1024]{2,1,0:T(8,128)(2,1)S(1)}, bf16[1,128,1024]{2,1,0:T(8,128)(2,1)}, u32[]{:S(2)}) copy-start(bf16[1,128,1024]{2,1,0:T(8,128)(2,1)} %param.15) | copy-start | bytes 786436
  94.4 14.3 %copy-start.10 = (bf16[4,2,32,1024]{3,2,1,0:T(8,128)(2,1)}, bf16[4,2,32,1024]{3,2,1,0:T(8,128)(2,1)S(1)}, u32[]{:S(2)}) copy-start(bf16[4,2,32,1024]{3,2,1,0:T(8,128)(2,1)S(1)} %collective-permute-done.3.refs_0_) | copy-start | bytes 1572868
  105.3 41.0 %collective-permute-start.5 = (bf16[4,128,1024]{2,1,0:T(8,128)(2,1)S(1)}, bf16[4,128,1024]{2,1,0:T(8,128)(2,1)S(1)}, u32[]{:S(2)}, u32[]{:S(2)}) collective-permute-start(bf16[4,128,1024]{2,1,0:T(8,128)(2,1)S(1)} %pad_maximum_fusion.kept), channel_id=1, source_target_pairs={{0,4},{2,6},{4,0},{6,2},{8,12},{10,14},{12,8},{14,10},{16,20},{18,... | collective-permute-start | bytes 3145736 | tf_op jit(solution)/shard_map/ppermute | solution.py:501
  107.2 2.7 copy-start.22
  108.7 33.1 %collective-permute-start.4 = (bf16[4,2,32,1024]{3,2,1,0:T(8,128)(2,1)S(1)}, bf16[4,2,32,1024]{3,2,1,0:T(8,128)(2,1)S(1)}, u32[]{:S(2)}, u32[]{:S(2)}) collective-permute-start(bf16[4,2,32,1024]{3,2,1,0:T(8,128)(2,1)S(1)} %slice_bitcast_fusion), channel_id=1, source_target_pairs={{0,4},{2,6},{4,0},{6,2},{8,12},{10,14},{12,8},{14,10},{16,20},{18,... | collective-permute-start | bytes 1572872 | tf_op jit(solution)/shard_map/ppermute | solution.py:501
  109.9 31.8 %copy-start.11 = (bf16[4,2,32,1024]{3,2,1,0:T(8,128)(2,1)S(1)}, bf16[4,2,32,1024]{3,2,1,0:T(8,128)(2,1)}, u32[]{:S(2)}) copy-start(bf16[4,2,32,1024]{3,2,1,0:T(8,128)(2,1)} %copy-done.10) | copy-start | bytes 1572868
  143.2 4.1 %copy-start.4 = (bf16[2,2,2,2,2,32,1024]{6,5,4,3,2,1,0:T(8,128)(2,1)}, bf16[2,2,2,2,2,32,1024]{6,5,4,3,2,1,0:T(8,128)(2,1)S(1)}, u32[]{:S(2)}) copy-start(bf16[2,2,2,2,2,32,1024]{6,5,4,3,2,1,0:T(8,128)(2,1)S(1)} %arrange.2) | copy-start | bytes 6291460
  167.2 27.4 %collective-permute-start.6 = (bf16[2,1,2,128,1024]{4,3,2,1,0:T(8,128)(2,1)}, bf16[2,1,2,128,1024]{4,3,2,1,0:T(8,128)(2,1)}, u32[]{:S(2)}, u32[]{:S(2)}) collective-permute-start(bf16[2,1,2,128,1024]{4,3,2,1,0:T(8,128)(2,1)} %constant_dynamic-slice_fusion.6), channel_id=1, source_target_pairs={{0,4},{2,6},{4,0},{6,2},{8,12},{10,14},{12,8},{14,10},{16,20},{18,... | collective-permute-start | bytes 3145736 | tf_op jit(solution)/shard_map/ppermute | solution.py:501
  172.1 3.1 %copy-start.5 = (bf16[2,2,2,2,2,32,1024]{6,5,4,3,2,1,0:T(8,128)(2,1)S(1)}, bf16[2,2,2,2,2,32,1024]{6,5,4,3,2,1,0:T(8,128)(2,1)}, u32[]{:S(2)}) copy-start(bf16[2,2,2,2,2,32,1024]{6,5,4,3,2,1,0:T(8,128)(2,1)} %copy-done.4) | copy-start | bytes 6291460
  173.2 37.8 %collective-permute-start.7 = (bf16[2,2,2,2,1,32,1024]{6,5,3,1,4,2,0:T(8,128)(2,1)}, bf16[2,2,2,2,1,32,1024]{6,5,3,1,4,2,0:T(8,128)(2,1)}, u32[]{:S(2)}, u32[]{:S(2)}) collective-permute-start(bf16[2,2,2,2,1,32,1024]{6,5,3,1,4,2,0:T(8,128)(2,1)} %copy.40), channel_id=1, source_target_pairs={{0,1},{1,0},{2,3},{3,2},{4,5},{5,4},{6,7},{7,6},{8,9},{9,8},{10,11... | collective-permute-start | bytes 3145736 | tf_op jit(solution)/shard_map/ppermute | solution.py:508
  177.8 16.8 %copy-start.25 = (bf16[1024,1024]{1,0:T(8,128)(2,1)S(1)}, bf16[1024,1024]{1,0:T(8,128)(2,1)}, u32[]{:S(2)}) copy-start(bf16[1024,1024]{1,0:T(8,128)(2,1)} %copy-done.24) | copy-start | bytes 6291460
  194.5 4.1 %copy-start.31 = (bf16[2,2,2,32,1024]{4,3,2,1,0:T(8,128)(2,1)S(1)}, bf16[2,2,2,32,1024]{4,3,2,1,0:T(8,128)(2,1)}, u32[]{:S(2)}) copy-start(bf16[2,2,2,32,1024]{4,3,2,1,0:T(8,128)(2,1)} %get-tuple-element.61) | copy-start | bytes 1572868
  197.3 13.7 %copy-start.18 = (bf16[2,2,2,2,1,32,1024]{6,5,4,3,2,1,0:T(8,128)(2,1)S(1)}, bf16[2,2,2,2,1,32,1024]{6,5,4,3,2,1,0:T(8,128)(2,1)}, u32[]{:S(2)}) copy-start(bf16[2,2,2,2,1,32,1024]{6,5,4,3,2,1,0:T(8,128)(2,1)} %get-tuple-element.94) | copy-start | bytes 3145732
  197.3 16.7 %collective-permute-start.9 = (bf16[2,1,1,128,1024]{4,3,2,1,0:T(8,128)(2,1)S(1)}, bf16[2,1,1,128,1024]{4,3,2,1,0:T(8,128)(2,1)}, u32[]{:S(2)}, u32[]{:S(2)}) collective-permute-start(bf16[2,1,1,128,1024]{4,3,2,1,0:T(8,128)(2,1)S(1)} %constant_dynamic-slice_fusion.2), channel_id=1, source_target_pairs={{0,1},{1,0},{2,3},{3,2},{4,5},{5,4},{6,7},{7,6},{8,9},{9,8},{10,11... | collective-permute-start | bytes 1572872 | tf_op jit(solution)/shard_map/ppermute | solution.py:508
  211.0 3.0 copy-start.20
  212.8 3.0 copy-start.1
  212.8 3.0 copy-start.6
  212.8 15.5 %collective-permute-start.8 = (bf16[2,2,1,2,1,32,1024]{6,5,3,1,4,2,0:T(8,128)(2,1)S(1)}, bf16[2,2,1,2,1,32,1024]{6,5,3,1,4,2,0:T(8,128)(2,1)S(1)}, u32[]{:S(2)}, u32[]{:S(2)}) collective-permute-start(bf16[2,2,1,2,1,32,1024]{6,5,3,1,4,2,0:T(8,128)(2,1)S(1)} %constant_dynamic-slice_fusion.3), channel_id=1, source_target_pairs={{0,4},{2,6},{4,0},{6,2},{8,12},{10,14},{12,8},{14,10},{16,20},{18,... | collective-permute-start | bytes 1572872 | tf_op jit(solution)/shard_map/ppermute | solution.py:501
  215.3 13.2 %collective-permute-start.10 = (bf16[1,1,128,1024]{3,2,1,0:T(8,128)(2,1)S(1)}, bf16[1,1,128,1024]{3,2,1,0:T(8,128)(2,1)S(1)}, u32[]{:S(2)}, u32[]{:S(2)}) collective-permute-start(bf16[1,1,128,1024]{3,2,1,0:T(8,128)(2,1)S(1)} %dynamic-slice_bitcast_fusion.1), channel_id=1, source_target_pairs={{0,16},{2,18},{4,20},{6,22},{8,24},{10,26},{12,28},{14,30},{16,0},... | collective-permute-start | bytes 786440 | tf_op jit(solution)/shard_map/ppermute | solution.py:501
  228.3 24.4 %copy-start.28 = (bf16[512,1024]{1,0:T(8,128)(2,1)S(1)}, bf16[512,1024]{1,0:T(8,128)(2,1)}, u32[]{:S(2)}) copy-start(bf16[512,1024]{1,0:T(8,128)(2,1)} %fusion.3) | copy-start | bytes 3145732
  252.6 13.0 %collective-permute-start.11 = (bf16[2,1,2,1,32,1024]{5,4,2,0,3,1:T(8,128)(2,1)S(1)}, bf16[2,1,2,1,32,1024]{5,4,2,0,3,1:T(8,128)(2,1)S(1)}, u32[]{:S(2)}, u32[]{:S(2)}) collective-permute-start(bf16[2,1,2,1,32,1024]{5,4,2,0,3,1:T(8,128)(2,1)S(1)} %dynamic-slice_bitcast_fusion), channel_id=1, source_target_pairs={{0,16},{2,18},{4,20},{6,22},{8,24},{10,26},{12,28},{14,30},{16,0},... | collective-permute-start | bytes 786440 | tf_op jit(solution)/shard_map/ppermute | solution.py:501
  265.7 36.6 %copy-start.13 = (bf16[128,1024]{1,0:T(8,128)(2,1)S(1)}, bf16[128,1024]{1,0:T(8,128)(2,1)}, u32[]{:S(2)}) copy-start(bf16[128,1024]{1,0:T(8,128)(2,1)} %copy-done.12) | copy-start | bytes 786436
  (20 other events, 33.6 us)
where the time goes:
time: 310 us; the launch traced here: 306 us
  Pallas kernels  215 us (69%)
  waiting for transfers between devices  25.4 us (8%)
  local copies, waits for them, and re-layouts  22 us (7%)
  matrix products  16.3 us (5%)
  other arithmetic  15.5 us (5%)
  starting transfers between devices  10.3 us (3%)
    pallas_call x4, Pallas kernels, exchange(): pl.pallas_call(to_heads_kernel if scatter else from_heads_kernel, out_sha...  68.9 us
    pallas_call x3, Pallas kernels, sum_rows(): pl.pallas_call(functools.partial(rows_kernel, step, gather, len(ins), len...  48.9 us
    pallas_call x1, Pallas kernels, start_gather(): pl.pallas_call(start_kernel, out_shape=(S(2, 2, 2, 2, 2, 32, 768), S(2, 2...  37.8 us
    pallas_call x1, Pallas kernels, reduce_all(): pl.pallas_call(reduce_kernel, out_shape=(S((q[0], 4 * q[1]), f32), S((o[0...  34.1 us
    ppermute x8, waiting for transfers between devices, flip(): return lax.ppermute(block, 'seq', [(s, s ^ bits) for s in range(16)])  25.4 us
    unnamed x86, local copies, waits for them, and re-layouts  11.9 us
    pallas_call x1, Pallas kernels, attend_back(): pl.pallas_call(attend_back_kernel, out_shape=jax.ShapeDtypeStruct(packed....  11.6 us
    pallas_call x1, Pallas kernels, attend(): pl.pallas_call(attend_kernel, out_shape=jax.ShapeDtypeStruct((packed.shap...  8.03 us
  transfers between devices with their start and end apart: 12, of which 3 were waited for; matrix products, arithmetic and copies ran while one was open for 12% of the time, Pallas kernels for 30%

commit v1 on v0

--- a/solution.py
+++ b/solution.py
@@ -1174,12 +1174,13 @@
     first = norm_rows(rows.astype(f32), vectors[4:5], vectors[8:9]).astype(bf16)
     up_two = cube_one(flip_x, up_one)
     projected = (dot_nn(first, wqkv) + jnp.concatenate([qk_shift, v_shift])).astype(bf16)
+    up_half = flip_y(up_two[:, 0])
     packed = exchange(after(projected, up_two, down_one), True, 1).reshape(8, 384, 128)
+    packed = after(packed, up_half)
     down_two = cube_one(flip_x, down_one)
-    up_half = flip_y(after(up_two, packed)[:, 0])
+    up_rest = flip_y(after(up_two, packed)[:, 1])
     attended = attend(valid[None], packed).reshape(2, 2, 2, 128, 128)
-    attended = exchange(after(attended, down_two, up_half), False, 2)
-    up_rest = flip_y(after(up_two, attended)[:, 1])
+    attended = exchange(after(attended, down_two, up_rest), False, 2)
     down_far = flip_y(after(down_two, attended))
     own_spot = lax.axis_index("seq") * 128 + jnp.arange(128, dtype=jnp.int32)
     grad_out = cotangent[0].astype(f32) * (own_spot < valid).astype(f32)[:, None]
@@ -1196,8 +1197,9 @@
         output_step, dot_nn(active, wd), (middle, grad_out, vectors), (low, line, line, line), True, 8)
     down_rows = down_rows.reshape(512, width)
     gw_down = contract_rows(active, down_rows).astype(bf16).reshape(2, 2, 2, 128, width)
-    down_term = flip_y(pick(gw_down, 1 - y, 1, True))
-    grad_up = (dot_nt(after(down_rows, gw_down), wd) * slope).astype(bf16)
+    down_send = pick(gw_down, 1 - y, 1, True)
+    down_term = flip_y(down_send)
+    grad_up = (dot_nt(after(down_rows, down_send), wd) * slope).astype(bf16)
     gw_up = contract_rows(third, grad_up).astype(bf16).reshape(2, 2, 2, 2, 2, 32, 1024)
     up_term = flip_x(pick(gw_up, 1 - x, 4, True))
     grad_middle, gain3, shift3, gain2, shift2, bias_out, branch_rows = sum_rows(
@@ -1206,18 +1208,18 @@
     branch_rows = branch_rows.reshape(512, width)
     grad_att = dot_nt(branch_rows, wo).astype(bf16)
     down_sum = add_low(pick(gw_down, y, 1, True), down_term)
+    up_sum = add_low(pick(gw_up, x, 4, True), up_term)
     down_term = flip_x(pick(down_sum, 1 - x, 2, True))
-    grad_packed = exchange(after(grad_att, down_sum), True, 3).reshape(8, 128, 128)
-    up_sum = add_low(pick(gw_up, x, 4, True), after(up_term, grad_packed))
     up_term = flip_y(pick(up_sum, 1 - y, 2, True))
+    grad_packed = exchange(after(grad_att, down_sum, up_sum), True, 3).reshape(8, 128, 128)
+    up_sum = add_low(pick(up_sum, y, 2, True), after(up_term, grad_packed))
+    up_term = flip_a(pick(up_sum, 1 - a, 0))
+    back = attend_back(valid[None], packed, grad_packed)
+
     down_sum = add_low(pick(down_sum, x, 2, True), after(down_term, grad_packed))
-    down_term = flip_a(pick(down_sum, 1 - a, 0))
-    back = attend_back(valid[None], packed, grad_packed)
-
-    up_sum = add_low(pick(up_sum, y, 2, True), up_term)
     gw_out = contract_rows(attended, branch_rows).astype(bf16).reshape(2, 2, 2, 32, width)
-    grad_qkv = exchange(after(back, up_sum, down_term).reshape(2, 2, 2, 384, 128), False, 4)
-    up_term = flip_a(pick(after(up_sum, grad_qkv), 1 - a, 0))
+    grad_qkv = exchange(after(back, up_term, down_sum).reshape(2, 2, 2, 384, 128), False, 4)
+    down_term = flip_a(pick(after(down_sum, grad_qkv), 1 - a, 0))
     gw_qkv = contract_rows(first, grad_qkv).astype(bf16).reshape(2, 2, 2, 2, 2, 32, 768)
     def sums(block):
         return jnp.sum(block.astype(f32), 0, keepdims=True)
@@ -1226,7 +1228,7 @@
     up_sum = (pick(up_sum, a, 0).astype(f32) + up_term.astype(f32)).astype(bf16).reshape(2, 2, 32, 1024)
     r_qkv, r_out, r_up, vectors, input_grad = reduce_all(
         gw_qkv, gw_out, up_sum, dot_nt(grad_qkv, wqkv), tokens[0], grad_middle, vectors, sums_of, 5)
-    r_down = (pick(down_sum, a, 0).astype(f32) + down_term.astype(f32)).reshape(128, width)
+    r_down = (pick(down_sum, a, 0).astype(f32) + after(down_term, vectors).astype(f32)).reshape(128, width)
     index = lax.axis_index("seq") * 2 + x
     small_up = lax.dynamic_slice(vectors, (12 + index // 8, index % 8 * 128), (1, 128)).reshape(128)
     vectors = lax.dynamic_slice(vectors, (0, index * 32), (12, 32))

time: 310 us -> 310 us (level)
  waiting for transfers between devices: 25.4 us -> 13.7 us
  Pallas kernels: 215 us -> 221 us
    ppermute x8, waiting for transfers between devices: 25.4 us -> 1.07 us  [flip(): return lax.ppermute(block, 'seq', [(s, s ^ bits) for s in range(16)])]
    ppermute x4, waiting for transfers between devices: 0.01 us -> 12.6 us  [flip_x(): return lax.ppermute(block, 'dp', [(0, 1), (1, 0)])]
    pallas_call x1, Pallas kernels: 34.1 us -> 39.3 us  [reduce_all(): pl.pallas_call(reduce_kernel, out_shape=(S((q[0], 4 * q[1]), f32), S((o[0...]
    unnamed x86 -> x88, local copies, waits for them, and re-layouts: 11.9 us -> 8.4 us
    pallas_call x4, Pallas kernels: 68.9 us -> 65.7 us  [exchange(): pl.pallas_call(to_heads_kernel if scatter else from_heads_kernel, out_sha...]
  transfers between devices with their start and end apart: 12 -> 12, of which waited for: 3 -> 3; matrix products, arithmetic and copies ran while one was open for 12% -> 11% of each run, Pallas kernels for 30% -> 43%
where the time goes in v1:
time: 310 us; the launch traced here: 305 us
  Pallas kernels  221 us (71%)
  local copies, waits for them, and re-layouts  23.1 us (7%)
  other arithmetic  17.6 us (6%)
  matrix products  17.4 us (6%)
  waiting for transfers between devices  13.7 us (4%)
  starting transfers between devices  10.5 us (3%)
    pallas_call x4, Pallas kernels, exchange(): pl.pallas_call(to_heads_kernel if scatter else from_heads_kernel, out_sha...  65.7 us
    pallas_call x3, Pallas kernels, sum_rows(): pl.pallas_call(functools.partial(rows_kernel, step, gather, len(ins), len...  50.4 us
    pallas_call x1, Pallas kernels, reduce_all(): pl.pallas_call(reduce_kernel, out_shape=(S((q[0], 4 * q[1]), f32), S((o[0...  39.3 us
    pallas_call x1, Pallas kernels, start_gather(): pl.pallas_call(start_kernel, out_shape=(S(2, 2, 2, 2, 2, 32, 768), S(2, 2...  37.8 us
    ppermute x4, waiting for transfers between devices, flip_x(): return lax.ppermute(block, 'dp', [(0, 1), (1, 0)])  12.6 us
    pallas_call x1, Pallas kernels, attend_back(): pl.pallas_call(attend_back_kernel, out_shape=jax.ShapeDtypeStruct(packed....  11.6 us
    unnamed x88, local copies, waits for them, and re-layouts  8.4 us
    pallas_call x1, Pallas kernels, attend(): pl.pallas_call(attend_kernel, out_shape=jax.ShapeDtypeStruct((packed.shap...  8.04 us
  transfers between devices with their start and end apart: 12, of which 3 were waited for; matrix products, arithmetic and copies ran while one was open for 11% of the time, Pallas kernels for 43%

profile of v1, /device:TPU:0, one launch (start us, length us, event | category | flops | bytes accessed | tf_op | source)
XLA Modules:
  0.0 305.2 jit_solution(12412171810088397848)
XLA Ops:
  0.7 1.4 pad_add_fusion.v_in
  2.0 37.8 %start_gather.1 = (bf16[2,2,2,2,2,32,768]{6,5,4,3,2,1,0:T(8,128)(2,1)}, bf16[2,2,2,32,1024]{4,3,2,1,0:T(8,128)(2,1)}, bf16[2,2,2,32,1024]{4,3,2,1,0:T(8,128)(2,1...) custom-call(bf16[32,3072]{1,0:T(8,128)(2,1)} %q_hbm.1, bf16[32,4096]{1,0:T(8,128)(2,1)} %u_hbm.1, ...), custom_call_target="tpu_custom_call" | custom-call | bytes 104857600 | tf_op jit(solution)/shard_map/start_gather/pallas_call | solution.py:981
  39.9 2.1 fusion.12
  42.0 1.5 collective-permute-start
  46.0 9.4 %collective-permute-done = bf16[2,2,2,32,1024]{4,3,2,0,1:T(8,128)(2,1)} collective-permute-done((bf16[2,2,2,32,1024]{4,3,2,0,1:T(8,128)(2,1)}, bf16[2,2,2,32,1024]{4,3,2,0,1:T(8,128)(2,1)}, u32[]{:S(2)}, u32[]{:S(2)}) %collective-permute-start) | collective-permute-done | bytes 524320 | tf_op jit(solution)/shard_map/ppermute | solution.py:508
  57.5 1.5 collective-permute-start.2
  59.0 1.9 add_convert_fusion.3.rows_ref
  61.8 1.4 collective-permute-start.3
  63.2 19.9 %to_heads.2 = bf16[2,2,2,384,128]{4,3,2,1,0:T(8,128)(2,1)} custom-call(bf16[512,768]{1,0:T(8,128)(2,1)} %add_convert_fusion.3.rows_ref), custom_call_target="tpu_custom_call" | custom-call | bytes 38400000 | tf_op jit(solution)/shard_map/to_heads/pallas_call | solution.py:378
  88.2 8.0 %attend.1 = bf16[8,128,128]{2,1,0:T(8,128)(2,1)S(1)} custom-call(s32[1]{0:T(128)} %bitcast.valid_ref, bf16[8,384,128]{2,1,0:T(8,128)(2,1)S(1)} %bitcast.120), custom_call_target="tpu_custom_call" | custom-call | tf_op jit(solution)/shard_map/attend/pallas_call | solution.py:476
  98.0 10.4 %from_heads.2 = bf16[512,256]{1,0:T(8,128)(2,1)} custom-call(bf16[2,2,2,128,128]{4,3,2,1,0:T(8,128)(2,1)} %bitcast.136), custom_call_target="tpu_custom_call" | custom-call | bytes 12800000 | tf_op jit(solution)/shard_map/from_heads/pallas_call | solution.py:378
  112.1 1.4 copy.33.kept
  113.5 1.6 fusion.15.part
  115.0 16.5 %sum_rows.3 = (f32[128,1024]{1,0:T(8,128)S(1)}, f32[128,1024]{1,0:T(8,128)S(1)}, bf16[4,128,1024]{2,1,0:T(8,128)(2,1)S(1)}) custom-call(f32[2,2,128,1024]{3,2,1,0:T(8,128)S(1)} %fusion.15.part, bf16[128,1024]{1,0:T(8,128)(2,1)S(1)} %bitcast.124, f32[12,1024]{1,0:T(8,128)S(1)} %convert_element_type.173.refs_1_.refs_2_.refs_3_.vectors), custom_call_target="tpu_custom_call" | custom-call | bytes 52428800 | tf_op jit(solution)/shard_map/sum_rows/pallas_call | solution.py:1098
  131.6 1.5 arrange.2
  133.1 3.1 %up_gelu.1 = (bf16[512,1024]{1,0:T(8,128)(2,1)S(1)}, f32[512,1024]{1,0:T(8,128)S(1)}) custom-call(bf16[512,1024]{1,0:T(8,128)(2,1)S(1)} %bitcast.140, bf16[1024,1024]{1,0:T(8,128)(2,1)S(1)} %bitcast.128, f32[1,1024]{1,0:T(1,128)S(1)} %convert.8.shift_ref), custom_call_target="tpu_custom_call" | custom-call | flops 1073741824 | bytes 25165824 | tf_op jit(solution)/shard_map/up_gelu/pallas_call | solution.py:590
  136.2 3.7 %arrange.3 = bf16[2,2,2,128,1024]{4,3,2,1,0:T(8,128)(2,1)S(1)} custom-call(s32[3]{0:T(128)S(1)} %pad_add_fusion.1.spot_ref, bf16[4,128,1024]{2,1,0:T(8,128)(2,1)S(1)} %pad_maximum_fusion.kept, bf16[4,128,1024]{2,1,0:T(8,128)(2,1)} %collective-permute-done.5.refs_0_), custom_call_target="tpu_custom_call" | custom-call | bytes 8388608 | tf_op jit(solution)/shard_map/arrange/pallas_call | solution.py:566
  141.2 17.0 %sum_rows.4 = (bf16[128,1024]{1,0:T(8,128)(2,1)S(1)}, f32[1,1024]{1,0:T(1,128)S(1)}, f32[1,1024]{1,0:T(1,128)S(1)}, f32[1,1024]{1,0:T(1,128)S(1)}, bf16[4,128,1024]{2,1,0:T(8,128)(2,1)S(1)}) custom-call(f32[2,2,128,1024]{3,2,1,0:T(8,128)S(1)} %fusion.16.part, f32[128,1024]{1,0:T(8,128)S(1)} %get-tuple-element.68.refs_0_, ...), custom_call_target="tpu_custom_call" | custom-call | bytes 52428800 | tf_op jit(solution)/shard_map/sum_rows/pallas_call | solution.py:1098
  161.2 1.3 convert_reduce_fusion
  166.7 1.5 fusion.3
  169.2 2.5 fusion.17
  171.8 16.9 %sum_rows.5 = (f32[128,1024]{1,0:T(8,128)S(1)}, f32[1,1024]{1,0:T(1,128)S(1)}, f32[1,1024]{1,0:T(1,128)S(1)}, f32[1,1024]{1,0:T(1,128)S(1)}, f32[1,1024]{1,0:T(1...) custom-call(f32[2,2,128,1024]{3,2,1,0:T(8,128)S(1)} %bitcast.127, ...), custom_call_target="tpu_custom_call" | custom-call | bytes 52428800 | tf_op jit(solution)/shard_map/sum_rows/pallas_call | solution.py:1098
  188.7 3.2 %collective-permute-done.7 = bf16[2,2,2,2,1,32,1024]{6,5,3,1,4,2,0:T(8,128)(2,1)} collective-permute-done((bf16[2,2,2,2,1,32,1024]{6,5,3,1,4,2,0:T(8,128)(2,1)}, bf16[2,2,2,2,1,32,1024]{6,5,3,1,4,2,0:T(8,128)(2,1)}, u32[]{:S(2)}, u32[]{:S(2)}) %collective-permute-start.7) | collective-permute-done | bytes 1048608 | tf_op jit(solution)/shard_map/ppermute | solution.py:508
  191.9 1.7 add_convert_fusion
  196.7 1.4 add_convert_fusion.1
  198.1 13.4 %to_heads.3 = bf16[2,2,2,128,128]{4,3,2,1,0:T(8,128)(2,1)} custom-call(bf16[512,256]{1,0:T(8,128)(2,1)} %convolution_convert_fusion.4.rows_ref), custom_call_target="tpu_custom_call" | custom-call | bytes 12800000 | tf_op jit(solution)/shard_map/to_heads/pallas_call | solution.py:378
  213.2 1.4 add_convert_fusion.5
  217.0 11.6 %attend_back.1 = bf16[8,384,128]{2,1,0:T(8,128)(2,1)S(1)} custom-call(s32[1]{0:T(128)} %bitcast.valid_ref, bf16[8,384,128]{2,1,0:T(8,128)(2,1)S(1)} %bitcast.121, bf16[8,128,128]{2,1,0:T(8,128)(2,1)S(1)} %bitcast.135), custom_call_target="tpu_custom_call" | custom-call | tf_op jit(solution)/shard_map/attend_back/pallas_call | solution.py:489
  230.4 22.0 %from_heads.3 = bf16[512,768]{1,0:T(8,128)(2,1)} custom-call(bf16[2,2,2,384,128]{4,3,2,1,0:T(8,128)(2,1)} %bitcast.122), custom_call_target="tpu_custom_call" | custom-call | bytes 38400000 | tf_op jit(solution)/shard_map/from_heads/pallas_call | solution.py:378
  253.7 2.3 convolution_convert_fusion.2
  256.2 2.4 fusion.18.part
  258.7 39.3 %reduce_all.1 = (f32[32,3072]{1,0:T(8,128)S(1)}, f32[32,1024]{1,0:T(8,128)S(1)}, f32[32,4096]{1,0:T(8,128)S(1)}, f32[16,1024]{1,0:T(8,128)S(1)}, bf16[128,1024]{1,0:T(8,128)(2,1)S(1)}) custom-call(bf16[2,2,2,2,2,32,768]{6,5,4,3,2,1,0:T(8,128)(2,1)S(1)} %bitcast.132, bf16[2,2,2,32,1024]{4,3,2,1,0:T(8,128)(2,1)S(1)} %bitcast.126, ...), custom_call_target="tpu_custom_call" | custom-call | tf_op jit(solution)/shard_map/reduce_all/pallas_call | solution.py:818
  (157 shorter events, 42.6 us)
Async XLA Ops:
  0.6 42.8 %copy-start.31 = (bf16[128,1024]{1,0:T(8,128)(2,1)S(1)}, bf16[128,1024]{1,0:T(8,128)(2,1)}, u32[]{:S(2)}) copy-start(bf16[128,1024]{1,0:T(8,128)(2,1)} %param.24) | copy-start | bytes 786436
  42.0 13.5 %collective-permute-start = (bf16[2,2,2,32,1024]{4,3,2,0,1:T(8,128)(2,1)}, bf16[2,2,2,32,1024]{4,3,2,0,1:T(8,128)(2,1)}, u32[]{:S(2)}, u32[]{:S(2)}) collective-permute-start(bf16[2,2,2,32,1024]{4,3,2,0,1:T(8,128)(2,1)} %get-tuple-element.98), channel_id=1, source_target_pairs={{0,1},{1,0},{2,3},{3,2},{4,5},{5,4},{6,7},{7,6},{8,9},{9,8},{10,11... | collective-permute-start | bytes 1572872 | tf_op jit(solution)/shard_map/ppermute | solution.py:508
  43.4 17.4 %collective-permute-start.1 = (bf16[128,1024]{1,0:T(8,128)(2,1)S(1)}, bf16[128,1024]{1,0:T(8,128)(2,1)S(1)}, u32[]{:S(2)}, u32[]{:S(2)}) collective-permute-start(bf16[128,1024]{1,0:T(8,128)(2,1)S(1)} %copy-done.31), channel_id=1, source_target_pairs={{0,16},{2,18},{4,20},{6,22},{8,24},{10,26},{12,28},{14,30},{16,0},... | collective-permute-start | bytes 786440 | tf_op jit(solution)/shard_map/ppermute | solution.py:501
  45.6 13.4 %copy-start.36 = (bf16[2,2,2,2,2,32,768]{6,5,4,3,2,1,0:T(8,128)(2,1)S(1)}, bf16[2,2,2,2,2,32,768]{6,5,4,3,2,1,0:T(8,128)(2,1)}, u32[]{:S(2)}) copy-start(bf16[2,2,2,2,2,32,768]{6,5,4,3,2,1,0:T(8,128)(2,1)} %get-tuple-element.56) | copy-start | bytes 4718596
  56.6 26.6 %copy-start.17 = (bf16[4,2,2,32,1024]{4,3,2,0,1:T(8,128)(2,1)}, bf16[4,2,2,32,1024]{4,3,2,0,1:T(8,128)(2,1)S(1)}, u32[]{:S(2)}) copy-start(bf16[4,2,2,32,1024]{4,3,2,0,1:T(8,128)(2,1)S(1)} %constant_dynamic-update-slice_fusion) | copy-start | bytes 3145732
  57.5 25.6 %collective-permute-start.2 = (bf16[4,2,32,1024]{3,2,1,0:T(8,128)(2,1)}, bf16[4,2,32,1024]{3,2,1,0:T(8,128)(2,1)S(1)}, u32[]{:S(2)}, u32[]{:S(2)}) collective-permute-start(bf16[4,2,32,1024]{3,2,1,0:T(8,128)(2,1)} %slice_bitcast_fusion), channel_id=1, source_target_pairs={{0,4},{2,6},{4,0},{6,2},{8,12},{10,14},{12,8},{14,10},{16,20},{18,... | collective-permute-start | bytes 1572872 | tf_op jit(solution)/shard_map/ppermute | solution.py:501
  60.9 24.1 %copy-start.38 = (s32[2]{0:T(128)S(1)}, s32[2]{0:T(128)}, u32[]{:S(2)}) copy-start(s32[2]{0:T(128)} %param.17) | copy-start | bytes 28
  60.9 24.7 %copy-start.39 = (s32[2]{0:T(128)S(1)}, s32[2]{0:T(128)}, u32[]{:S(2)}) copy-start(s32[2]{0:T(128)} %param.16) | copy-start | bytes 28
  60.9 26.0 %copy-start.32 = (bf16[128,1024]{1,0:T(8,128)(2,1)}, bf16[128,1024]{1,0:T(8,128)(2,1)S(1)}, u32[]{:S(2)}) copy-start(bf16[128,1024]{1,0:T(8,128)(2,1)S(1)} %collective-permute-done.1) | copy-start | bytes 786436
  61.8 25.1 %collective-permute-start.3 = (bf16[2,128,1024]{2,1,0:T(8,128)(2,1)}, bf16[2,128,1024]{2,1,0:T(8,128)(2,1)}, u32[]{:S(2)}, u32[]{:S(2)}) collective-permute-start(bf16[2,128,1024]{2,1,0:T(8,128)(2,1)} %pad_maximum_fusion.1), channel_id=1, source_target_pairs={{0,1},{1,0},{2,3},{3,2},{4,5},{5,4},{6,7},{7,6},{8,9},{9,8},{10,11... | collective-permute-start | bytes 1572872 | tf_op jit(solution)/shard_map/ppermute | solution.py:508
  83.1 5.1 %copy-start = (bf16[2,2,2,384,128]{4,3,2,1,0:T(8,128)(2,1)S(1)}, bf16[2,2,2,384,128]{4,3,2,1,0:T(8,128)(2,1)}, u32[]{:S(2)}) copy-start(bf16[2,2,2,384,128]{4,3,2,1,0:T(8,128)(2,1)} %to_heads.2) | copy-start | bytes 2359300
  83.1 5.1 %copy-start.9 = (bf16[4,2,32,1024]{3,2,1,0:T(8,128)(2,1)}, bf16[4,2,32,1024]{3,2,1,0:T(8,128)(2,1)S(1)}, u32[]{:S(2)}) copy-start(bf16[4,2,32,1024]{3,2,1,0:T(8,128)(2,1)S(1)} %collective-permute-done.2.refs_0_) | copy-start | bytes 1572868
  84.0 25.2 %copy-start.29 = (f32[32,12,32]{2,0,1:T(8,128)S(1)}, f32[32,12,32]{2,0,1:T(8,128)}, u32[]{:S(2)}) copy-start(f32[32,12,32]{2,0,1:T(8,128)} %copy-done.28) | copy-start | bytes 147460
  84.0 14.0 %collective-permute-start.4 = (bf16[4,2,32,1024]{3,2,1,0:T(8,128)(2,1)}, bf16[4,2,32,1024]{3,2,1,0:T(8,128)(2,1)S(1)}, u32[]{:S(2)}, u32[]{:S(2)}) collective-permute-start(bf16[4,2,32,1024]{3,2,1,0:T(8,128)(2,1)} %slice_bitcast_fusion.1), channel_id=1, source_target_pairs={{0,4},{2,6},{4,0},{6,2},{8,12},{10,14},{12,8},{14,10},{16,20},{18,... | collective-permute-start | bytes 1572872 | tf_op jit(solution)/shard_map/ppermute | solution.py:501
  98.0 13.0 %copy-start.11 = (bf16[4,2,32,1024]{3,2,1,0:T(8,128)(2,1)}, bf16[4,2,32,1024]{3,2,1,0:T(8,128)(2,1)S(1)}, u32[]{:S(2)}) copy-start(bf16[4,2,32,1024]{3,2,1,0:T(8,128)(2,1)S(1)} %collective-permute-done.4.refs_1_) | copy-start | bytes 1572868
  108.4 5.0 %copy-start.22 = (bf16[512,256]{1,0:T(8,128)(2,1)S(1)}, bf16[512,256]{1,0:T(8,128)(2,1)}, u32[]{:S(2)}) copy-start(bf16[512,256]{1,0:T(8,128)(2,1)} %from_heads.2) | copy-start | bytes 786436
  108.4 27.8 %collective-permute-start.5 = (bf16[4,128,1024]{2,1,0:T(8,128)(2,1)S(1)}, bf16[4,128,1024]{2,1,0:T(8,128)(2,1)}, u32[]{:S(2)}, u32[]{:S(2)}) collective-permute-start(bf16[4,128,1024]{2,1,0:T(8,128)(2,1)S(1)} %pad_maximum_fusion.kept), channel_id=1, source_target_pairs={{0,4},{2,6},{4,0},{6,2},{8,12},{10,14},{12,8},{14,10},{16,20},{18,... | collective-permute-start | bytes 3145736 | tf_op jit(solution)/shard_map/ppermute | solution.py:501
  113.4 18.1 %copy-start.10 = (bf16[4,2,32,1024]{3,2,1,0:T(8,128)(2,1)S(1)}, bf16[4,2,32,1024]{3,2,1,0:T(8,128)(2,1)}, u32[]{:S(2)}) copy-start(bf16[4,2,32,1024]{3,2,1,0:T(8,128)(2,1)} %copy-done.9) | copy-start | bytes 1572868
  113.4 18.1 %copy-start.12 = (bf16[4,2,32,1024]{3,2,1,0:T(8,128)(2,1)S(1)}, bf16[4,2,32,1024]{3,2,1,0:T(8,128)(2,1)}, u32[]{:S(2)}) copy-start(bf16[4,2,32,1024]{3,2,1,0:T(8,128)(2,1)} %copy-done.11) | copy-start | bytes 1572868
  133.1 6.8 %copy-start.3 = (bf16[2,2,2,2,2,32,1024]{6,5,4,3,2,1,0:T(8,128)(2,1)}, bf16[2,2,2,2,2,32,1024]{6,5,4,3,2,1,0:T(8,128)(2,1)S(1)}, u32[]{:S(2)}) copy-start(bf16[2,2,2,2,2,32,1024]{6,5,4,3,2,1,0:T(8,128)(2,1)S(1)} %arrange.2) | copy-start | bytes 6291460
  166.1 25.7 %collective-permute-start.7 = (bf16[2,2,2,2,1,32,1024]{6,5,3,1,4,2,0:T(8,128)(2,1)}, bf16[2,2,2,2,1,32,1024]{6,5,3,1,4,2,0:T(8,128)(2,1)}, u32[]{:S(2)}, u32[]{:S(2)}) collective-permute-start(bf16[2,2,2,2,1,32,1024]{6,5,3,1,4,2,0:T(8,128)(2,1)} %copy.40), channel_id=1, source_target_pairs={{0,1},{1,0},{2,3},{3,2},{4,5},{5,4},{6,7},{7,6},{8,9},{9,8},{10,11... | collective-permute-start | bytes 3145736 | tf_op jit(solution)/shard_map/ppermute | solution.py:508
  168.1 28.6 %collective-permute-start.6 = (bf16[2,1,2,128,1024]{4,3,2,1,0:T(8,128)(2,1)}, bf16[2,1,2,128,1024]{4,3,2,1,0:T(8,128)(2,1)S(1)}, u32[]{:S(2)}, u32[]{:S(2)}) collective-permute-start(bf16[2,1,2,128,1024]{4,3,2,1,0:T(8,128)(2,1)} %constant_dynamic-slice_fusion.6), channel_id=1, source_target_pairs={{0,4},{2,6},{4,0},{6,2},{8,12},{10,14},{12,8},{14,10},{16,20},{18,... | collective-permute-start | bytes 3145736 | tf_op jit(solution)/shard_map/ppermute | solution.py:501
  171.7 20.1 %copy-start.18 = (bf16[2,2,2,2,1,32,1024]{6,5,4,3,2,1,0:T(8,128)(2,1)S(1)}, bf16[2,2,2,2,1,32,1024]{6,5,4,3,2,1,0:T(8,128)(2,1)}, u32[]{:S(2)}) copy-start(bf16[2,2,2,2,1,32,1024]{6,5,4,3,2,1,0:T(8,128)(2,1)} %get-tuple-element.96) | copy-start | bytes 3145732
  188.7 5.8 %copy-start.13 = (f32[128,1024]{1,0:T(8,128)}, f32[128,1024]{1,0:T(8,128)S(1)}, u32[]{:S(2)}) copy-start(f32[128,1024]{1,0:T(8,128)S(1)} %get-tuple-element.80.grad_middle) | copy-start | bytes 1572868
  193.6 18.0 %copy-start.19 = (bf16[2,2,2,2,1,32,1024]{6,5,3,1,4,2,0:T(8,128)(2,1)}, bf16[2,2,2,2,1,32,1024]{6,5,3,1,4,2,0:T(8,128)(2,1)S(1)}, u32[]{:S(2)}) copy-start(bf16[2,2,2,2,1,32,1024]{6,5,3,1,4,2,0:T(8,128)(2,1)S(1)} %add_convert_fusion) | copy-start | bytes 3145732
  194.4 18.8 %collective-permute-start.8 = (bf16[2,2,1,2,1,32,1024]{6,5,3,1,4,2,0:T(8,128)(2,1)}, bf16[2,2,1,2,1,32,1024]{6,5,3,1,4,2,0:T(8,128)(2,1)}, u32[]{:S(2)}, u32[]{:S(2)}) collective-permute-start(bf16[2,2,1,2,1,32,1024]{6,5,3,1,4,2,0:T(8,128)(2,1)} %constant_dynamic-slice_fusion.3), channel_id=1, source_target_pairs={{0,4},{2,6},{4,0},{6,2},{8,12},{10,14},{12,8},{14,10},{16,20},{18,... | collective-permute-start | bytes 1572872 | tf_op jit(solution)/shard_map/ppermute | solution.py:501
  211.6 5.0 %copy-start.23 = (bf16[512,256]{1,0:T(8,128)(2,1)S(1)}, bf16[512,256]{1,0:T(8,128)(2,1)}, u32[]{:S(2)}) copy-start(bf16[512,256]{1,0:T(8,128)(2,1)} %from_heads.2) | copy-start | bytes 786436
  212.7 16.8 %collective-permute-start.10 = (bf16[2,1,1,128,1024]{4,3,2,1,0:T(8,128)(2,1)S(1)}, bf16[2,1,1,128,1024]{4,3,2,1,0:T(8,128)(2,1)S(1)}, u32[]{:S(2)}, u32[]{:S(2)}) collective-permute-start(bf16[2,1,1,128,1024]{4,3,2,1,0:T(8,128)(2,1)S(1)} %constant_dynamic-slice_fusion.2), channel_id=1, source_target_pairs={{0,1},{1,0},{2,3},{3,2},{4,5},{5,4},{6,7},{7,6},{8,9},{9,8},{10,11... | collective-permute-start | bytes 1572872 | tf_op jit(solution)/shard_map/ppermute | solution.py:508
  214.6 14.9 %copy-start.20 = (bf16[2,1,2,128,1024]{4,3,2,1,0:T(8,128)(2,1)S(1)}, bf16[2,1,2,128,1024]{4,3,2,1,0:T(8,128)(2,1)}, u32[]{:S(2)}) copy-start(bf16[2,1,2,128,1024]{4,3,2,1,0:T(8,128)(2,1)} %add_convert_fusion.1) | copy-start | bytes 3145732
  215.4 14.3 %collective-permute-start.9 = (bf16[2,1,2,1,32,1024]{5,4,2,0,3,1:T(8,128)(2,1)S(1)}, bf16[2,1,2,1,32,1024]{5,4,2,0,3,1:T(8,128)(2,1)S(1)}, u32[]{:S(2)}, u32[]{:S(2)}) collective-permute-start(bf16[2,1,2,1,32,1024]{5,4,2,0,3,1:T(8,128)(2,1)S(1)} %dynamic-slice_bitcast_fusion.1), channel_id=1, source_target_pairs={{0,16},{2,18},{4,20},{6,22},{8,24},{10,26},{12,28},{14,30},{16,0},... | collective-permute-start | bytes 786440 | tf_op jit(solution)/shard_map/ppermute | solution.py:501
  229.5 24.2 %copy-start.30 = (bf16[512,1024]{1,0:T(8,128)(2,1)S(1)}, bf16[512,1024]{1,0:T(8,128)(2,1)}, u32[]{:S(2)}) copy-start(bf16[512,1024]{1,0:T(8,128)(2,1)} %fusion.3) | copy-start | bytes 3145732
  256.1 44.4 %collective-permute-start.11 = (bf16[1,1,128,1024]{3,2,1,0:T(8,128)(2,1)S(1)}, bf16[1,1,128,1024]{3,2,1,0:T(8,128)(2,1)S(1)}, u32[]{:S(2)}, u32[]{:S(2)}) collective-permute-start(bf16[1,1,128,1024]{3,2,1,0:T(8,128)(2,1)S(1)} %dynamic-slice_bitcast_fusion), channel_id=1, source_target_pairs={{0,16},{2,18},{4,20},{6,22},{8,24},{10,26},{12,28},{14,30},{16,0},... | collective-permute-start | bytes 786440 | tf_op jit(solution)/shard_map/ppermute | solution.py:501
  (21 other events, 48.0 us)

commit v2 on v0

--- a/solution.py
+++ b/solution.py
@@ -520,33 +520,29 @@
     return jnp.concatenate([block, flip_one(block)], 0)
 
 
-def arrange_kernel(spot_ref, kept, *refs):
-    out = refs[-1]
-    i = pl.program_id(0)
-    wide = len(out.shape) == 7
-
-    @pl.when(i < 4)
-    def _():
-        if wide:
+def arrange_kernel(spot_ref, kept, received, out):
+    def put(block):
+        if len(out.shape) == 7:
             for j in range(2):
                 for k in range(2):
-                    out[0, j, 0, k, 0] = kept[0, j, k]
+                    out[0, j, 0, k, 0] = block[0, j, k]
         else:
-            out[0, 0, 0] = kept[0]
-
-    @pl.when(i >= 4)
+            out[0, 0, 0] = block[0]
+
+    @pl.when(pl.program_id(0) < 4)
     def _():
-        if wide:
-            for j in range(2):
-                for k in range(2):
-                    out[0, j, 0, k, 0] = refs[j][0, k]
-        else:
-            out[0, 0, 0] = refs[0][0]
-
-
-def arrange(spot, kept, *received):
+        put(kept)
+
+    @pl.when(pl.program_id(0) >= 4)
+    def _():
+        put(received)
+
+
+def arrange(spot, y_first, kept, received):
     def coords(i, r):
-        return lax.rem(r[0] + i % 2, 2), lax.rem(r[1] + i // 4, 2), lax.rem(r[2] + (i // 2) % 2, 2)
+        second, first = i // 4, (i // 2) % 2
+        y, x = (first, second) if y_first else (second, first)
+        return lax.rem(r[0] + i % 2, 2), lax.rem(r[1] + y, 2), lax.rem(r[2] + x, 2)
 
     shape = kept.shape
 
@@ -567,12 +563,12 @@
         arrange_kernel,
         out_shape=jax.ShapeDtypeStruct(out_shape, kept.dtype),
         grid_spec=pltpu.PrefetchScalarGridSpec(
-            num_scalar_prefetch=1, grid=(8,), in_specs=[spec(kept, 0)] + [spec(block, 4) for block in received],
+            num_scalar_prefetch=1, grid=(8,), in_specs=[spec(kept, 0), spec(received, 4)],
             out_specs=pl.BlockSpec(out_block, out_place)),
         compiler_params=pltpu.CompilerParams(vmem_limit_bytes=32 << 20),
         cost_estimate=pl.CostEstimate(flops=0, bytes_accessed=8 << 20, transcendentals=0),
         name="arrange",
-    )(spot, kept, *received)
+    )(spot, kept, received)
 
 
 def up_kernel(rows_ref, w_ref, shift_ref, active_ref, slope_ref):
@@ -1175,12 +1171,10 @@
     up_two = cube_one(flip_x, up_one)
     projected = (dot_nn(first, wqkv) + jnp.concatenate([qk_shift, v_shift])).astype(bf16)
     packed = exchange(after(projected, up_two, down_one), True, 1).reshape(8, 384, 128)
-    down_two = cube_one(flip_x, down_one)
-    up_half = flip_y(after(up_two, packed)[:, 0])
+    down_two = cube_one(flip_y, after(down_one, packed))
     attended = attend(valid[None], packed).reshape(2, 2, 2, 128, 128)
-    attended = exchange(after(attended, down_two, up_half), False, 2)
-    up_rest = flip_y(after(up_two, attended)[:, 1])
-    down_far = flip_y(after(down_two, attended))
+    attended = exchange(after(attended, down_two), False, 2)
+    up_far, down_far = flip_y(after(up_two, attended)), flip_x(after(down_two, attended))
     own_spot = lax.axis_index("seq") * 128 + jnp.arange(128, dtype=jnp.int32)
     grad_out = cotangent[0].astype(f32) * (own_spot < valid).astype(f32)[:, None]
     S = jax.ShapeDtypeStruct
@@ -1189,9 +1183,9 @@
         attended_step, dot_nn(attended, wo), (tokens[0], vectors),
         (wide, wide), True, 7)
     third = third.reshape(512, width)
-    wu = arrange(spot, up_two, up_half, up_rest).reshape(width, 1024)
+    wu = arrange(spot, False, up_two, up_far).reshape(width, 1024)
     active, slope = up_gelu(third, wu, up_shift.reshape(1, 1024))
-    wd = arrange(spot, down_two, after(down_far, active)).reshape(1024, width)
+    wd = arrange(spot, True, down_two, after(down_far, active)).reshape(1024, width)
     output, gain4, shift4, bias_down, down_rows = sum_rows(
         output_step, dot_nn(active, wd), (middle, grad_out, vectors), (low, line, line, line), True, 8)
     down_rows = down_rows.reshape(512, width)

time: 310 us -> 301 us (0.971)
  waiting for transfers between devices: 25.4 us -> 15.3 us
  Pallas kernels: 215 us -> 219 us
    ppermute x8 -> x7, waiting for transfers between devices: 25.4 us -> 14.8 us  [flip(): return lax.ppermute(block, 'seq', [(s, s ^ bits) for s in range(16)])]
    pallas_call x2, Pallas kernels: 2.49 us -> 7.84 us  [arrange(): pl.pallas_call(arrange_kernel, out_shape=jax.ShapeDtypeStruct(out_shape,...]
    unnamed x86 -> x74, local copies, waits for them, and re-layouts: 11.9 us -> 11.6 us
  transfers between devices with their start and end apart: 12 -> 11, of which waited for: 3 -> 5; matrix products, arithmetic and copies ran while one was open for 12% -> 11% of each run, Pallas kernels for 30% -> 24%
where the time goes in v2:
time: 301 us; the launch traced here: 297 us
  Pallas kernels  219 us (73%)
  local copies, waits for them, and re-layouts  19.9 us (7%)
  matrix products  17.8 us (6%)
  waiting for transfers between devices  15.3 us (5%)
  other arithmetic  14.5 us (5%)
  starting transfers between devices  9.38 us (3%)
    pallas_call x4, Pallas kernels, exchange(): pl.pallas_call(to_heads_kernel if scatter else from_heads_kernel, out_sha...  66.8 us
    pallas_call x3, Pallas kernels, sum_rows(): pl.pallas_call(functools.partial(rows_kernel, step, gather, len(ins), len...  49.8 us
    pallas_call x1, Pallas kernels, start_gather(): pl.pallas_call(start_kernel, out_shape=(S(2, 2, 2, 2, 2, 32, 768), S(2, 2...  37.8 us
    pallas_call x1, Pallas kernels, reduce_all(): pl.pallas_call(reduce_kernel, out_shape=(S((q[0], 4 * q[1]), f32), S((o[0...  33.5 us
    ppermute x7, waiting for transfers between devices, flip(): return lax.ppermute(block, 'seq', [(s, s ^ bits) for s in range(16)])  14.8 us
    pallas_call x1, Pallas kernels, attend_back(): pl.pallas_call(attend_back_kernel, out_shape=jax.ShapeDtypeStruct(packed....  11.6 us
    unnamed x74, local copies, waits for them, and re-layouts  11.6 us
    pallas_call x1, Pallas kernels, attend(): pl.pallas_call(attend_kernel, out_shape=jax.ShapeDtypeStruct((packed.shap...  8.04 us
  transfers between devices with their start and end apart: 11, of which 5 were waited for; matrix products, arithmetic and copies ran while one was open for 11% of the time, Pallas kernels for 24%

profile of v2, /device:TPU:0, one launch (start us, length us, event | category | flops | bytes accessed | tf_op | source)
XLA Modules:
  0.0 297.2 jit_solution(13892006993945582226)
XLA Ops:
  0.6 1.3 pad_add_fusion.v_in
  2.0 37.8 %start_gather.1 = (bf16[2,2,2,2,2,32,768]{6,5,4,3,2,1,0:T(8,128)(2,1)}, bf16[2,2,2,32,1024]{4,3,2,1,0:T(8,128)(2,1)}, bf16[2,2,2,32,1024]{4,3,2,1,0:T(8,128)(2,1...) custom-call(bf16[32,3072]{1,0:T(8,128)(2,1)} %q_hbm.1, bf16[32,4096]{1,0:T(8,128)(2,1)} %u_hbm.1, ...), custom_call_target="tpu_custom_call" | custom-call | bytes 104857600 | tf_op jit(solution)/shard_map/start_gather/pallas_call | solution.py:977
  39.9 1.6 collective-permute-start
  46.1 1.9 add_convert_fusion.3.rows_ref
  48.0 4.8 %collective-permute-done.1 = bf16[128,1024]{1,0:T(8,128)(2,1)S(1)} collective-permute-done((bf16[128,1024]{1,0:T(8,128)(2,1)}, bf16[128,1024]{1,0:T(8,128)(2,1)S(1)}, u32[]{:S(2)}, u32[]{:S(2)}) %collective-permute-start.1) | collective-permute-done | bytes 262176 | tf_op jit(solution)/shard_map/ppermute | solution.py:501
  53.4 23.0 %to_heads.2 = bf16[2,2,2,384,128]{4,3,2,1,0:T(8,128)(2,1)} custom-call(bf16[512,768]{1,0:T(8,128)(2,1)} %add_convert_fusion.3.rows_ref), custom_call_target="tpu_custom_call" | custom-call | bytes 38400000 | tf_op jit(solution)/shard_map/to_heads/pallas_call | solution.py:378
  80.1 8.0 %attend.1 = bf16[8,128,128]{2,1,0:T(8,128)(2,1)S(1)} custom-call(s32[1]{0:T(128)} %bitcast.valid_ref, bf16[8,384,128]{2,1,0:T(8,128)(2,1)S(1)} %bitcast.116), custom_call_target="tpu_custom_call" | custom-call | tf_op jit(solution)/shard_map/attend/pallas_call | solution.py:476
  88.2 2.0 collective-permute-done.2
  91.3 10.0 %from_heads.2 = bf16[512,256]{1,0:T(8,128)(2,1)} custom-call(bf16[2,2,2,128,128]{4,3,2,1,0:T(8,128)(2,1)} %bitcast.132), custom_call_target="tpu_custom_call" | custom-call | bytes 12800000 | tf_op jit(solution)/shard_map/from_heads/pallas_call | solution.py:378
  101.4 1.4 collective-permute-start.3
  102.8 1.6 collective-permute-start.4
  107.3 1.6 fusion.14.part
  108.8 16.3 %sum_rows.3 = (f32[128,1024]{1,0:T(8,128)S(1)}, f32[128,1024]{1,0:T(8,128)S(1)}, bf16[4,128,1024]{2,1,0:T(8,128)(2,1)S(1)}) custom-call(f32[2,2,128,1024]{3,2,1,0:T(8,128)S(1)} %fusion.14.part, bf16[128,1024]{1,0:T(8,128)(2,1)S(1)} %bitcast.120, f32[12,1024]{1,0:T(8,128)S(1)} %convert_element_type.173.refs_1_.refs_2_.refs_3_.vectors), custom_call_target="tpu_custom_call" | custom-call | bytes 52428800 | tf_op jit(solution)/shard_map/sum_rows/pallas_call | solution.py:1094
  126.0 4.1 %arrange.2 = bf16[2,2,2,2,2,32,1024]{6,5,4,3,2,1,0:T(8,128)(2,1)S(1)} custom-call(s32[3]{0:T(128)S(1)} %pad_add_fusion.1.spot_ref, bf16[4,2,2,32,1024]{4,3,2,1,0:T(8,128)(2,1)S(1)} %constant_dynamic-update-slice_fusion.kept, bf16[4,2,2,32,1024]{4,3,2,1,0:T(8,128)(2,1)} %collective-permute-done.3.received), custom_call_target="tpu_custom_call" | custom-call | bytes 8388608 | tf_op jit(solution)/shard_map/arrange/pallas_call | solution.py:562
  130.1 3.1 %up_gelu.1 = (bf16[512,1024]{1,0:T(8,128)(2,1)S(1)}, f32[512,1024]{1,0:T(8,128)S(1)}) custom-call(bf16[512,1024]{1,0:T(8,128)(2,1)S(1)} %bitcast.136, bf16[1024,1024]{1,0:T(8,128)(2,1)S(1)} %bitcast.124, f32[1,1024]{1,0:T(1,128)S(1)} %convert.8.shift_ref), custom_call_target="tpu_custom_call" | custom-call | flops 1073741824 | bytes 25165824 | tf_op jit(solution)/shard_map/up_gelu/pallas_call | solution.py:586
  133.3 3.7 %arrange.3 = bf16[2,2,2,128,1024]{4,3,2,1,0:T(8,128)(2,1)S(1)} custom-call(s32[3]{0:T(128)S(1)} %pad_add_fusion.1.spot_ref, bf16[4,128,1024]{2,1,0:T(8,128)(2,1)S(1)} %constant_dynamic-update-slice_fusion.2.kept, bf16[4,128,1024]{2,1,0:T(8,128)(2,1)} %collective-permute-done.4.received), custom_call_target="tpu_custom_call" | custom-call | bytes 8388608 | tf_op jit(solution)/shard_map/arrange/pallas_call | solution.py:562
  138.3 17.0 %sum_rows.4 = (bf16[128,1024]{1,0:T(8,128)(2,1)S(1)}, f32[1,1024]{1,0:T(1,128)S(1)}, f32[1,1024]{1,0:T(1,128)S(1)}, f32[1,1024]{1,0:T(1,128)S(1)}, bf16[4,128,1024]{2,1,0:T(8,128)(2,1)S(1)}) custom-call(f32[2,2,128,1024]{3,2,1,0:T(8,128)S(1)} %fusion.15.part, f32[128,1024]{1,0:T(8,128)S(1)} %get-tuple-element.67.refs_0_, ...), custom_call_target="tpu_custom_call" | custom-call | bytes 52428800 | tf_op jit(solution)/shard_map/sum_rows/pallas_call | solution.py:1094
  155.2 1.3 convolution_convert_fusion.1
  158.3 1.3 convert_reduce_fusion
  163.1 1.8 collective-permute-start.6
  164.9 1.4 fusion.3
  166.4 2.9 fusion.16
  169.3 16.6 %sum_rows.5 = (f32[128,1024]{1,0:T(8,128)S(1)}, f32[1,1024]{1,0:T(1,128)S(1)}, f32[1,1024]{1,0:T(1,128)S(1)}, f32[1,1024]{1,0:T(1,128)S(1)}, f32[1,1024]{1,0:T(1...) custom-call(f32[2,2,128,1024]{3,2,1,0:T(8,128)S(1)} %bitcast.123, ...), custom_call_target="tpu_custom_call" | custom-call | bytes 52428800 | tf_op jit(solution)/shard_map/sum_rows/pallas_call | solution.py:1094
  186.0 1.7 add_convert_fusion.1
  191.3 11.3 %to_heads.3 = bf16[2,2,2,128,128]{4,3,2,1,0:T(8,128)(2,1)} custom-call(bf16[512,256]{1,0:T(8,128)(2,1)} %convolution_convert_fusion.4.rows_ref), custom_call_target="tpu_custom_call" | custom-call | bytes 12800000 | tf_op jit(solution)/shard_map/to_heads/pallas_call | solution.py:378
  202.6 1.7 add_convert_fusion
  207.5 11.6 %attend_back.1 = bf16[8,384,128]{2,1,0:T(8,128)(2,1)S(1)} custom-call(s32[1]{0:T(128)} %bitcast.valid_ref, bf16[8,384,128]{2,1,0:T(8,128)(2,1)S(1)} %bitcast.117, bf16[8,128,128]{2,1,0:T(8,128)(2,1)S(1)} %bitcast.131), custom_call_target="tpu_custom_call" | custom-call | tf_op jit(solution)/shard_map/attend_back/pallas_call | solution.py:489
  220.9 22.5 %from_heads.3 = bf16[512,768]{1,0:T(8,128)(2,1)} custom-call(bf16[2,2,2,384,128]{4,3,2,1,0:T(8,128)(2,1)} %bitcast.118), custom_call_target="tpu_custom_call" | custom-call | bytes 38400000 | tf_op jit(solution)/shard_map/from_heads/pallas_call | solution.py:378
  243.6 2.3 convolution_convert_fusion.2
  246.0 2.4 fusion.17.part
  249.4 7.9 %collective-permute-done.10 = bf16[2,1,2,1,32,1024]{5,4,2,0,3,1:T(8,128)(2,1)S(1)} collective-permute-done((bf16[2,1,2,1,32,1024]{5,4,2,0,3,1:T(8,128)(2,1)S(1)}, bf16[2,1,2,1,32,1024]{5,4,2,0,3,1:T(8,128)(2,1)S(1)}, u32[]{:S(2)}, u32[]{:S(2)}) %collective-permute-start.10) | collective-permute-done | bytes 262176 | tf_op jit(solution)/shard_map/ppermute | solution.py:501
  257.3 33.5 %reduce_all.1 = (f32[32,3072]{1,0:T(8,128)S(1)}, f32[32,1024]{1,0:T(8,128)S(1)}, f32[32,4096]{1,0:T(8,128)S(1)}, f32[16,1024]{1,0:T(8,128)S(1)}, bf16[128,1024]{1,0:T(8,128)(2,1)S(1)}) custom-call(bf16[2,2,2,2,2,32,768]{6,5,4,3,2,1,0:T(8,128)(2,1)S(1)} %bitcast.128, bf16[2,2,2,32,1024]{4,3,2,1,0:T(8,128)(2,1)S(1)} %bitcast.122, ...), custom_call_target="tpu_custom_call" | custom-call | tf_op jit(solution)/shard_map/reduce_all/pallas_call | solution.py:814
  (137 shorter events, 36.0 us)
Async XLA Ops:
  39.8 3.9 %copy-start.11 = (bf16[4,128,1024]{2,1,0:T(8,128)(2,1)S(1)}, bf16[4,128,1024]{2,1,0:T(8,128)(2,1)}, u32[]{:S(2)}) copy-start(bf16[4,128,1024]{2,1,0:T(8,128)(2,1)} %get-tuple-element.53) | copy-start | bytes 3145732
  39.8 13.0 %collective-permute-start.1 = (bf16[128,1024]{1,0:T(8,128)(2,1)}, bf16[128,1024]{1,0:T(8,128)(2,1)S(1)}, u32[]{:S(2)}, u32[]{:S(2)}) collective-permute-start(bf16[128,1024]{1,0:T(8,128)(2,1)} %param.24), channel_id=1, source_target_pairs={{0,16},{2,18},{4,20},{6,22},{8,24},{10,26},{12,28},{14,30},{16,0},... | collective-permute-start | bytes 786440 | tf_op jit(solution)/shard_map/ppermute | solution.py:501
  39.9 13.5 %collective-permute-start = (bf16[2,2,2,32,1024]{4,3,2,1,0:T(8,128)(2,1)}, bf16[2,2,2,32,1024]{4,3,2,1,0:T(8,128)(2,1)S(1)}, u32[]{:S(2)}, u32[]{:S(2)}) collective-permute-start(bf16[2,2,2,32,1024]{4,3,2,1,0:T(8,128)(2,1)} %get-tuple-element.56), channel_id=1, source_target_pairs={{0,1},{1,0},{2,3},{3,2},{4,5},{5,4},{6,7},{7,6},{8,9},{9,8},{10,11... | collective-permute-start | bytes 1572872 | tf_op jit(solution)/shard_map/ppermute | solution.py:508
  42.5 2.7 copy-start.22
  46.1 6.7 %copy-start.26 = (bf16[128,1024]{1,0:T(8,128)(2,1)S(1)}, bf16[128,1024]{1,0:T(8,128)(2,1)}, u32[]{:S(2)}) copy-start(bf16[128,1024]{1,0:T(8,128)(2,1)} %param.24) | copy-start | bytes 786436
  48.0 29.1 %copy-start.31 = (s32[2]{0:T(128)S(1)}, s32[2]{0:T(128)}, u32[]{:S(2)}) copy-start(s32[2]{0:T(128)} %param.17) | copy-start | bytes 28
  48.0 29.7 %copy-start.32 = (s32[2]{0:T(128)S(1)}, s32[2]{0:T(128)}, u32[]{:S(2)}) copy-start(s32[2]{0:T(128)} %param.16) | copy-start | bytes 28
  53.4 51.8 %copy-start.23 = (f32[32,12,32]{2,0,1:T(8,128)S(1)}, f32[32,12,32]{2,0,1:T(8,128)}, u32[]{:S(2)}) copy-start(f32[32,12,32]{2,0,1:T(8,128)} %copy-done.22) | copy-start | bytes 147460
  76.5 13.8 %collective-permute-start.2 = (bf16[2,128,1024]{2,1,0:T(8,128)(2,1)S(1)}, bf16[2,128,1024]{2,1,0:T(8,128)(2,1)}, u32[]{:S(2)}, u32[]{:S(2)}) collective-permute-start(bf16[2,128,1024]{2,1,0:T(8,128)(2,1)S(1)} %pad_maximum_fusion), channel_id=1, source_target_pairs={{0,4},{2,6},{4,0},{6,2},{8,12},{10,14},{12,8},{14,10},{16,20},{18,... | collective-permute-start | bytes 1572872 | tf_op jit(solution)/shard_map/ppermute | solution.py:501
  88.2 3.1 %copy-start.6 = (bf16[8,128,128]{2,1,0:T(8,128)(2,1)}, bf16[8,128,128]{2,1,0:T(8,128)(2,1)S(1)}, u32[]{:S(2)}) copy-start(bf16[8,128,128]{2,1,0:T(8,128)(2,1)S(1)} %attend.1) | copy-start | bytes 786436
  101.4 7.4 %copy-start.3 = (bf16[1,128,1024]{2,1,0:T(8,128)(2,1)S(1)}, bf16[1,128,1024]{2,1,0:T(8,128)(2,1)}, u32[]{:S(2)}) copy-start(bf16[1,128,1024]{2,1,0:T(8,128)(2,1)} %param.14) | copy-start | bytes 786436
  101.4 24.6 %collective-permute-start.3 = (bf16[4,2,2,32,1024]{4,3,2,1,0:T(8,128)(2,1)S(1)}, bf16[4,2,2,32,1024]{4,3,2,1,0:T(8,128)(2,1)}, u32[]{:S(2)}, u32[]{:S(2)}) collective-permute-start(bf16[4,2,2,32,1024]{4,3,2,1,0:T(8,128)(2,1)S(1)} %constant_dynamic-update-slice_fusion.kept), channel_id=1, source_target_pairs={{0,4},{2,6},{4,0},{6,2},{8,12},{10,14},{12,8},{14,10},{16,20},{18,... | collective-permute-start | bytes 3145736 | tf_op jit(solution)/shard_map/ppermute | solution.py:501
  102.8 30.4 %collective-permute-start.4 = (bf16[4,128,1024]{2,1,0:T(8,128)(2,1)S(1)}, bf16[4,128,1024]{2,1,0:T(8,128)(2,1)}, u32[]{:S(2)}, u32[]{:S(2)}) collective-permute-start(bf16[4,128,1024]{2,1,0:T(8,128)(2,1)S(1)} %constant_dynamic-update-slice_fusion.2.kept), channel_id=1, source_target_pairs={{0,1},{1,0},{2,3},{3,2},{4,5},{5,4},{6,7},{7,6},{8,9},{9,8},{10,11... | collective-permute-start | bytes 3145736 | tf_op jit(solution)/shard_map/ppermute | solution.py:508
  130.1 6.8 %copy-start.4 = (bf16[2,2,2,2,2,32,1024]{6,5,4,3,2,1,0:T(8,128)(2,1)}, bf16[2,2,2,2,2,32,1024]{6,5,4,3,2,1,0:T(8,128)(2,1)S(1)}, u32[]{:S(2)}) copy-start(bf16[2,2,2,2,2,32,1024]{6,5,4,3,2,1,0:T(8,128)(2,1)S(1)} %arrange.2) | copy-start | bytes 6291460
  156.6 3.0 %copy-start.18 = (bf16[1024,1024]{1,0:T(8,128)(2,1)}, bf16[1024,1024]{1,0:T(8,128)(2,1)S(1)}, u32[]{:S(2)}) copy-start(bf16[1024,1024]{1,0:T(8,128)(2,1)S(1)} %convolution_convert_fusion.1) | copy-start | bytes 6291460
  157.7 28.2 %collective-permute-start.5 = (bf16[2,1,2,128,1024]{4,3,2,1,0:T(8,128)(2,1)}, bf16[2,1,2,128,1024]{4,3,2,1,0:T(8,128)(2,1)}, u32[]{:S(2)}, u32[]{:S(2)}) collective-permute-start(bf16[2,1,2,128,1024]{4,3,2,1,0:T(8,128)(2,1)} %constant_dynamic-slice_fusion.6), channel_id=1, source_target_pairs={{0,4},{2,6},{4,0},{6,2},{8,12},{10,14},{12,8},{14,10},{16,20},{18,... | collective-permute-start | bytes 3145736 | tf_op jit(solution)/shard_map/ppermute | solution.py:501
  162.1 2.8 copy-start.12
  163.1 39.5 %collective-permute-start.6 = (bf16[2,2,2,2,1,32,1024]{6,5,3,1,4,2,0:T(8,128)(2,1)}, bf16[2,2,2,2,1,32,1024]{6,5,3,1,4,2,0:T(8,128)(2,1)}, u32[]{:S(2)}, u32[]{:S(2)}) collective-permute-start(bf16[2,2,2,2,1,32,1024]{6,5,3,1,4,2,0:T(8,128)(2,1)} %copy.34), channel_id=1, source_target_pairs={{0,1},{1,0},{2,3},{3,2},{4,5},{5,4},{6,7},{7,6},{8,9},{9,8},{10,11... | collective-permute-start | bytes 3145736 | tf_op jit(solution)/shard_map/ppermute | solution.py:508
  166.4 3.0 copy-start.8
  169.3 16.7 %copy-start.19 = (bf16[1024,1024]{1,0:T(8,128)(2,1)S(1)}, bf16[1024,1024]{1,0:T(8,128)(2,1)}, u32[]{:S(2)}) copy-start(bf16[1024,1024]{1,0:T(8,128)(2,1)} %copy-done.18) | copy-start | bytes 6291460
  185.9 4.2 %copy-start.25 = (bf16[2,2,2,32,1024]{4,3,2,1,0:T(8,128)(2,1)S(1)}, bf16[2,2,2,32,1024]{4,3,2,1,0:T(8,128)(2,1)}, u32[]{:S(2)}) copy-start(bf16[2,2,2,32,1024]{4,3,2,1,0:T(8,128)(2,1)} %get-tuple-element.61) | copy-start | bytes 1572868
  188.6 14.0 %copy-start.13 = (bf16[2,2,2,2,1,32,1024]{6,5,4,3,2,1,0:T(8,128)(2,1)S(1)}, bf16[2,2,2,2,1,32,1024]{6,5,4,3,2,1,0:T(8,128)(2,1)}, u32[]{:S(2)}) copy-start(bf16[2,2,2,2,1,32,1024]{6,5,4,3,2,1,0:T(8,128)(2,1)} %get-tuple-element.94) | copy-start | bytes 3145732
  189.5 16.0 %collective-permute-start.8 = (bf16[2,1,1,128,1024]{4,3,2,1,0:T(8,128)(2,1)}, bf16[2,1,1,128,1024]{4,3,2,1,0:T(8,128)(2,1)}, u32[]{:S(2)}, u32[]{:S(2)}) collective-permute-start(bf16[2,1,1,128,1024]{4,3,2,1,0:T(8,128)(2,1)} %constant_dynamic-slice_fusion.2), channel_id=1, source_target_pairs={{0,1},{1,0},{2,3},{3,2},{4,5},{5,4},{6,7},{7,6},{8,9},{9,8},{10,11... | collective-permute-start | bytes 1572872 | tf_op jit(solution)/shard_map/ppermute | solution.py:508
  202.6 2.8 copy-start.15
  204.4 3.1 %copy-start.1 = (bf16[2,2,2,384,128]{4,3,2,1,0:T(8,128)(2,1)S(1)}, bf16[2,2,2,384,128]{4,3,2,1,0:T(8,128)(2,1)}, u32[]{:S(2)}) copy-start(bf16[2,2,2,384,128]{4,3,2,1,0:T(8,128)(2,1)} %to_heads.2) | copy-start | bytes 2359300
  204.4 3.1 %copy-start.5 = (bf16[2,2,2,128,128]{4,3,2,1,0:T(8,128)(2,1)S(1)}, bf16[2,2,2,128,128]{4,3,2,1,0:T(8,128)(2,1)}, u32[]{:S(2)}) copy-start(bf16[2,2,2,128,128]{4,3,2,1,0:T(8,128)(2,1)} %to_heads.3) | copy-start | bytes 786436
  204.4 15.6 %collective-permute-start.7 = (bf16[2,2,1,2,1,32,1024]{6,5,3,1,4,2,0:T(8,128)(2,1)S(1)}, bf16[2,2,1,2,1,32,1024]{6,5,3,1,4,2,0:T(8,128)(2,1)S(1)}, u32[]{:S(2)}, u32[]{:S(2)}) collective-permute-start(bf16[2,2,1,2,1,32,1024]{6,5,3,1,4,2,0:T(8,128)(2,1)S(1)} %constant_dynamic-slice_fusion.3), channel_id=1, source_target_pairs={{0,4},{2,6},{4,0},{6,2},{8,12},{10,14},{12,8},{14,10},{16,20},{18,... | collective-permute-start | bytes 1572872 | tf_op jit(solution)/shard_map/ppermute | solution.py:501
  206.7 13.5 %collective-permute-start.9 = (bf16[1,1,128,1024]{3,2,1,0:T(8,128)(2,1)S(1)}, bf16[1,1,128,1024]{3,2,1,0:T(8,128)(2,1)S(1)}, u32[]{:S(2)}, u32[]{:S(2)}) collective-permute-start(bf16[1,1,128,1024]{3,2,1,0:T(8,128)(2,1)S(1)} %dynamic-slice_bitcast_fusion.1), channel_id=1, source_target_pairs={{0,16},{2,18},{4,20},{6,22},{8,24},{10,26},{12,28},{14,30},{16,0},... | collective-permute-start | bytes 786440 | tf_op jit(solution)/shard_map/ppermute | solution.py:501
  220.0 23.6 %copy-start.24 = (bf16[512,1024]{1,0:T(8,128)(2,1)S(1)}, bf16[512,1024]{1,0:T(8,128)(2,1)}, u32[]{:S(2)}) copy-start(bf16[512,1024]{1,0:T(8,128)(2,1)} %fusion.3) | copy-start | bytes 3145732
  243.5 13.7 %collective-permute-start.10 = (bf16[2,1,2,1,32,1024]{5,4,2,0,3,1:T(8,128)(2,1)S(1)}, bf16[2,1,2,1,32,1024]{5,4,2,0,3,1:T(8,128)(2,1)S(1)}, u32[]{:S(2)}, u32[]{:S(2)}) collective-permute-start(bf16[2,1,2,1,32,1024]{5,4,2,0,3,1:T(8,128)(2,1)S(1)} %dynamic-slice_bitcast_fusion), channel_id=1, source_target_pairs={{0,16},{2,18},{4,20},{6,22},{8,24},{10,26},{12,28},{14,30},{16,0},... | collective-permute-start | bytes 786440 | tf_op jit(solution)/shard_map/ppermute | solution.py:501
  245.9 2.6 copy-start.21
  257.3 36.0 %copy-start.10 = (bf16[128,1024]{1,0:T(8,128)(2,1)S(1)}, bf16[128,1024]{1,0:T(8,128)(2,1)}, u32[]{:S(2)}) copy-start(bf16[128,1024]{1,0:T(8,128)(2,1)} %copy-done.9) | copy-start | bytes 786436
  (12 other events, 17.9 us)

commit v3 on v2

--- a/solution.py
+++ b/solution.py
@@ -522,48 +522,50 @@
 
 def arrange_kernel(spot_ref, kept, received, out):
     def put(block):
-        if len(out.shape) == 7:
-            for j in range(2):
-                for k in range(2):
-                    out[0, j, 0, k, 0] = block[0, j, k]
-        else:
-            out[0, 0, 0] = block[0]
-
-    @pl.when(pl.program_id(0) < 4)
+        for step in range(2):
+            a = lax.rem(spot_ref[0] + step, 2)
+            if len(out.shape) == 7:
+                for j in range(2):
+                    for k in range(2):
+                        out[a, j, 0, k, 0] = block[step, j, k]
+            else:
+                out[a, 0, 0] = block[step]
+
+    @pl.when(pl.program_id(0) < 2)
     def _():
         put(kept)
 
-    @pl.when(pl.program_id(0) >= 4)
+    @pl.when(pl.program_id(0) >= 2)
     def _():
         put(received)
 
 
 def arrange(spot, y_first, kept, received):
     def coords(i, r):
-        second, first = i // 4, (i // 2) % 2
+        second, first = i // 2, i % 2
         y, x = (first, second) if y_first else (second, first)
-        return lax.rem(r[0] + i % 2, 2), lax.rem(r[1] + y, 2), lax.rem(r[2] + x, 2)
+        return lax.rem(r[1] + y, 2), lax.rem(r[2] + x, 2)
 
     shape = kept.shape
 
     def spec(block, low):
         rest = (0,) * (block.ndim - 1)
-        return pl.BlockSpec((1,) + block.shape[1:], lambda i, r: (jnp.clip(i - low, 0, 3),) + rest)
+        return pl.BlockSpec((2,) + block.shape[1:], lambda i, r: (jnp.clip(i - low, 0, 1),) + rest)
 
     if len(shape) == 5:
         def out_place(i, r):
-            a, y, x = coords(i, r)
-            return a, 0, y, 0, x, 0, 0
-        out_block, out_shape = (1, 2, 1, 2, 1) + shape[3:], (2,) * 5 + shape[3:]
+            y, x = coords(i, r)
+            return 0, 0, y, 0, x, 0, 0
+        out_block, out_shape = (2, 2, 1, 2, 1) + shape[3:], (2,) * 5 + shape[3:]
     else:
         def out_place(i, r):
-            return coords(i, r) + (0, 0)
-        out_block, out_shape = (1, 1, 1) + shape[1:], (2, 2, 2) + shape[1:]
+            return (0,) + coords(i, r) + (0, 0)
+        out_block, out_shape = (2, 1, 1) + shape[1:], (2, 2, 2) + shape[1:]
     return pl.pallas_call(
         arrange_kernel,
         out_shape=jax.ShapeDtypeStruct(out_shape, kept.dtype),
         grid_spec=pltpu.PrefetchScalarGridSpec(
-            num_scalar_prefetch=1, grid=(8,), in_specs=[spec(kept, 0), spec(received, 4)],
+            num_scalar_prefetch=1, grid=(4,), in_specs=[spec(kept, 0), spec(received, 2)],
             out_specs=pl.BlockSpec(out_block, out_place)),
         compiler_params=pltpu.CompilerParams(vmem_limit_bytes=32 << 20),
         cost_estimate=pl.CostEstimate(flops=0, bytes_accessed=8 << 20, transcendentals=0),

time: 301 us -> 300 us (level)
  transfers between devices with their start and end apart: 11 -> 11, of which waited for: 5 -> 5; matrix products, arithmetic and copies ran while one was open for 11% -> 12% of each run, Pallas kernels for 24% -> 24%
where the time goes in v3:
time: 300 us; the launch traced here: 295 us
  Pallas kernels  217 us (72%)
  local copies, waits for them, and re-layouts  19.9 us (7%)
  matrix products  17.8 us (6%)
  waiting for transfers between devices  15.3 us (5%)
  other arithmetic  14.5 us (5%)
  starting transfers between devices  9.37 us (3%)
    pallas_call x4, Pallas kernels, exchange(): pl.pallas_call(to_heads_kernel if scatter else from_heads_kernel, out_sha...  66.9 us
    pallas_call x3, Pallas kernels, sum_rows(): pl.pallas_call(functools.partial(rows_kernel, step, gather, len(ins), len...  49.8 us
    pallas_call x1, Pallas kernels, start_gather(): pl.pallas_call(start_kernel, out_shape=(S(2, 2, 2, 2, 2, 32, 768), S(2, 2...  37.8 us
    pallas_call x1, Pallas kernels, reduce_all(): pl.pallas_call(reduce_kernel, out_shape=(S((q[0], 4 * q[1]), f32), S((o[0...  33.5 us
    ppermute x7, waiting for transfers between devices, flip(): return lax.ppermute(block, 'seq', [(s, s ^ bits) for s in range(16)])  14.8 us
    pallas_call x1, Pallas kernels, attend_back(): pl.pallas_call(attend_back_kernel, out_shape=jax.ShapeDtypeStruct(packed....  11.6 us
    unnamed x74, local copies, waits for them, and re-layouts  11.6 us
    pallas_call x1, Pallas kernels, attend(): pl.pallas_call(attend_kernel, out_shape=jax.ShapeDtypeStruct((packed.shap...  8.04 us
  transfers between devices with their start and end apart: 11, of which 5 were waited for; matrix products, arithmetic and copies ran while one was open for 12% of the time, Pallas kernels for 24%

profile of v3, /device:TPU:0, one launch (start us, length us, event | category | flops | bytes accessed | tf_op | source)
XLA Modules:
  0.0 295.4 jit_solution(7396433594577074438)
XLA Ops:
  0.6 1.3 pad_add_fusion.v_in
  2.0 37.8 %start_gather.1 = (bf16[2,2,2,2,2,32,768]{6,5,4,3,2,1,0:T(8,128)(2,1)}, bf16[2,2,2,32,1024]{4,3,2,1,0:T(8,128)(2,1)}, bf16[2,2,2,32,1024]{4,3,2,1,0:T(8,128)(2,1...) custom-call(bf16[32,3072]{1,0:T(8,128)(2,1)} %q_hbm.1, bf16[32,4096]{1,0:T(8,128)(2,1)} %u_hbm.1, ...), custom_call_target="tpu_custom_call" | custom-call | bytes 104857600 | tf_op jit(solution)/shard_map/start_gather/pallas_call | solution.py:979
  39.9 1.6 collective-permute-start
  46.1 1.9 add_convert_fusion.3.rows_ref
  48.0 4.8 %collective-permute-done.1 = bf16[128,1024]{1,0:T(8,128)(2,1)S(1)} collective-permute-done((bf16[128,1024]{1,0:T(8,128)(2,1)}, bf16[128,1024]{1,0:T(8,128)(2,1)S(1)}, u32[]{:S(2)}, u32[]{:S(2)}) %collective-permute-start.1) | collective-permute-done | bytes 262176 | tf_op jit(solution)/shard_map/ppermute | solution.py:501
  53.4 23.0 %to_heads.2 = bf16[2,2,2,384,128]{4,3,2,1,0:T(8,128)(2,1)} custom-call(bf16[512,768]{1,0:T(8,128)(2,1)} %add_convert_fusion.3.rows_ref), custom_call_target="tpu_custom_call" | custom-call | bytes 38400000 | tf_op jit(solution)/shard_map/to_heads/pallas_call | solution.py:378
  80.1 8.0 %attend.1 = bf16[8,128,128]{2,1,0:T(8,128)(2,1)S(1)} custom-call(s32[1]{0:T(128)} %bitcast.valid_ref, bf16[8,384,128]{2,1,0:T(8,128)(2,1)S(1)} %bitcast.116), custom_call_target="tpu_custom_call" | custom-call | tf_op jit(solution)/shard_map/attend/pallas_call | solution.py:476
  88.2 2.0 collective-permute-done.2
  91.3 10.0 %from_heads.2 = bf16[512,256]{1,0:T(8,128)(2,1)} custom-call(bf16[2,2,2,128,128]{4,3,2,1,0:T(8,128)(2,1)} %bitcast.132), custom_call_target="tpu_custom_call" | custom-call | bytes 12800000 | tf_op jit(solution)/shard_map/from_heads/pallas_call | solution.py:378
  101.4 1.4 collective-permute-start.3
  102.8 1.6 collective-permute-start.4
  107.3 1.6 fusion.14.part
  108.8 16.3 %sum_rows.3 = (f32[128,1024]{1,0:T(8,128)S(1)}, f32[128,1024]{1,0:T(8,128)S(1)}, bf16[4,128,1024]{2,1,0:T(8,128)(2,1)S(1)}) custom-call(f32[2,2,128,1024]{3,2,1,0:T(8,128)S(1)} %fusion.14.part, bf16[128,1024]{1,0:T(8,128)(2,1)S(1)} %bitcast.120, f32[12,1024]{1,0:T(8,128)S(1)} %convert_element_type.173.refs_1_.refs_2_.refs_3_.vectors), custom_call_target="tpu_custom_call" | custom-call | bytes 52428800 | tf_op jit(solution)/shard_map/sum_rows/pallas_call | solution.py:1096
  126.0 3.1 %arrange.2 = bf16[2,2,2,2,2,32,1024]{6,5,4,3,2,1,0:T(8,128)(2,1)S(1)} custom-call(s32[3]{0:T(128)S(1)} %pad_add_fusion.1.spot_ref, bf16[4,2,2,32,1024]{4,3,2,1,0:T(8,128)(2,1)S(1)} %constant_dynamic-update-slice_fusion.kept, bf16[4,2,2,32,1024]{4,3,2,1,0:T(8,128)(2,1)} %collective-permute-done.3.received), custom_call_target="tpu_custom_call" | custom-call | bytes 8388608 | tf_op jit(solution)/shard_map/arrange/pallas_call | solution.py:564
  129.1 3.1 %up_gelu.1 = (bf16[512,1024]{1,0:T(8,128)(2,1)S(1)}, f32[512,1024]{1,0:T(8,128)S(1)}) custom-call(bf16[512,1024]{1,0:T(8,128)(2,1)S(1)} %bitcast.136, bf16[1024,1024]{1,0:T(8,128)(2,1)S(1)} %bitcast.124, f32[1,1024]{1,0:T(1,128)S(1)} %convert.8.shift_ref), custom_call_target="tpu_custom_call" | custom-call | flops 1073741824 | bytes 25165824 | tf_op jit(solution)/shard_map/up_gelu/pallas_call | solution.py:588
  132.2 3.1 %arrange.3 = bf16[2,2,2,128,1024]{4,3,2,1,0:T(8,128)(2,1)S(1)} custom-call(s32[3]{0:T(128)S(1)} %pad_add_fusion.1.spot_ref, bf16[4,128,1024]{2,1,0:T(8,128)(2,1)S(1)} %constant_dynamic-update-slice_fusion.2.kept, bf16[4,128,1024]{2,1,0:T(8,128)(2,1)} %collective-permute-done.4.received), custom_call_target="tpu_custom_call" | custom-call | bytes 8388608 | tf_op jit(solution)/shard_map/arrange/pallas_call | solution.py:564
  136.5 17.0 %sum_rows.4 = (bf16[128,1024]{1,0:T(8,128)(2,1)S(1)}, f32[1,1024]{1,0:T(1,128)S(1)}, f32[1,1024]{1,0:T(1,128)S(1)}, f32[1,1024]{1,0:T(1,128)S(1)}, bf16[4,128,1024]{2,1,0:T(8,128)(2,1)S(1)}) custom-call(f32[2,2,128,1024]{3,2,1,0:T(8,128)S(1)} %fusion.15.part, f32[128,1024]{1,0:T(8,128)S(1)} %get-tuple-element.67.refs_0_, ...), custom_call_target="tpu_custom_call" | custom-call | bytes 52428800 | tf_op jit(solution)/shard_map/sum_rows/pallas_call | solution.py:1096
  153.5 1.3 convolution_convert_fusion.1
  156.6 1.3 convert_reduce_fusion
  161.4 1.8 collective-permute-start.6
  163.2 1.4 fusion.3
  164.7 2.9 fusion.16
  167.6 16.6 %sum_rows.5 = (f32[128,1024]{1,0:T(8,128)S(1)}, f32[1,1024]{1,0:T(1,128)S(1)}, f32[1,1024]{1,0:T(1,128)S(1)}, f32[1,1024]{1,0:T(1,128)S(1)}, f32[1,1024]{1,0:T(1...) custom-call(f32[2,2,128,1024]{3,2,1,0:T(8,128)S(1)} %bitcast.123, ...), custom_call_target="tpu_custom_call" | custom-call | bytes 52428800 | tf_op jit(solution)/shard_map/sum_rows/pallas_call | solution.py:1096
  184.3 1.7 add_convert_fusion.1
  189.6 11.3 %to_heads.3 = bf16[2,2,2,128,128]{4,3,2,1,0:T(8,128)(2,1)} custom-call(bf16[512,256]{1,0:T(8,128)(2,1)} %convolution_convert_fusion.4.rows_ref), custom_call_target="tpu_custom_call" | custom-call | bytes 12800000 | tf_op jit(solution)/shard_map/to_heads/pallas_call | solution.py:378
  200.9 1.7 add_convert_fusion
  205.8 11.6 %attend_back.1 = bf16[8,384,128]{2,1,0:T(8,128)(2,1)S(1)} custom-call(s32[1]{0:T(128)} %bitcast.valid_ref, bf16[8,384,128]{2,1,0:T(8,128)(2,1)S(1)} %bitcast.117, bf16[8,128,128]{2,1,0:T(8,128)(2,1)S(1)} %bitcast.131), custom_call_target="tpu_custom_call" | custom-call | tf_op jit(solution)/shard_map/attend_back/pallas_call | solution.py:489
  219.2 22.5 %from_heads.3 = bf16[512,768]{1,0:T(8,128)(2,1)} custom-call(bf16[2,2,2,384,128]{4,3,2,1,0:T(8,128)(2,1)} %bitcast.118), custom_call_target="tpu_custom_call" | custom-call | bytes 38400000 | tf_op jit(solution)/shard_map/from_heads/pallas_call | solution.py:378
  241.9 2.3 convolution_convert_fusion.2
  244.2 2.4 fusion.17.part
  247.7 7.9 %collective-permute-done.10 = bf16[2,1,2,1,32,1024]{5,4,2,0,3,1:T(8,128)(2,1)S(1)} collective-permute-done((bf16[2,1,2,1,32,1024]{5,4,2,0,3,1:T(8,128)(2,1)S(1)}, bf16[2,1,2,1,32,1024]{5,4,2,0,3,1:T(8,128)(2,1)S(1)}, u32[]{:S(2)}, u32[]{:S(2)}) %collective-permute-start.10) | collective-permute-done | bytes 262176 | tf_op jit(solution)/shard_map/ppermute | solution.py:501
  255.6 33.5 %reduce_all.1 = (f32[32,3072]{1,0:T(8,128)S(1)}, f32[32,1024]{1,0:T(8,128)S(1)}, f32[32,4096]{1,0:T(8,128)S(1)}, f32[16,1024]{1,0:T(8,128)S(1)}, bf16[128,1024]{1,0:T(8,128)(2,1)S(1)}) custom-call(bf16[2,2,2,2,2,32,768]{6,5,4,3,2,1,0:T(8,128)(2,1)S(1)} %bitcast.128, bf16[2,2,2,32,1024]{4,3,2,1,0:T(8,128)(2,1)S(1)} %bitcast.122, ...), custom_call_target="tpu_custom_call" | custom-call | tf_op jit(solution)/shard_map/reduce_all/pallas_call | solution.py:816
  (137 shorter events, 36.0 us)
Async XLA Ops:
  39.8 3.9 %copy-start.11 = (bf16[4,128,1024]{2,1,0:T(8,128)(2,1)S(1)}, bf16[4,128,1024]{2,1,0:T(8,128)(2,1)}, u32[]{:S(2)}) copy-start(bf16[4,128,1024]{2,1,0:T(8,128)(2,1)} %get-tuple-element.53) | copy-start | bytes 3145732
  39.8 13.0 %collective-permute-start.1 = (bf16[128,1024]{1,0:T(8,128)(2,1)}, bf16[128,1024]{1,0:T(8,128)(2,1)S(1)}, u32[]{:S(2)}, u32[]{:S(2)}) collective-permute-start(bf16[128,1024]{1,0:T(8,128)(2,1)} %param.24), channel_id=1, source_target_pairs={{0,16},{2,18},{4,20},{6,22},{8,24},{10,26},{12,28},{14,30},{16,0},... | collective-permute-start | bytes 786440 | tf_op jit(solution)/shard_map/ppermute | solution.py:501
  39.9 13.5 %collective-permute-start = (bf16[2,2,2,32,1024]{4,3,2,1,0:T(8,128)(2,1)}, bf16[2,2,2,32,1024]{4,3,2,1,0:T(8,128)(2,1)S(1)}, u32[]{:S(2)}, u32[]{:S(2)}) collective-permute-start(bf16[2,2,2,32,1024]{4,3,2,1,0:T(8,128)(2,1)} %get-tuple-element.56), channel_id=1, source_target_pairs={{0,1},{1,0},{2,3},{3,2},{4,5},{5,4},{6,7},{7,6},{8,9},{9,8},{10,11... | collective-permute-start | bytes 1572872 | tf_op jit(solution)/shard_map/ppermute | solution.py:508
  42.5 2.7 copy-start.22
  46.1 6.7 %copy-start.26 = (bf16[128,1024]{1,0:T(8,128)(2,1)S(1)}, bf16[128,1024]{1,0:T(8,128)(2,1)}, u32[]{:S(2)}) copy-start(bf16[128,1024]{1,0:T(8,128)(2,1)} %param.24) | copy-start | bytes 786436
  48.0 29.1 %copy-start.31 = (s32[2]{0:T(128)S(1)}, s32[2]{0:T(128)}, u32[]{:S(2)}) copy-start(s32[2]{0:T(128)} %param.17) | copy-start | bytes 28
  48.0 29.7 %copy-start.32 = (s32[2]{0:T(128)S(1)}, s32[2]{0:T(128)}, u32[]{:S(2)}) copy-start(s32[2]{0:T(128)} %param.16) | copy-start | bytes 28
  53.4 51.8 %copy-start.23 = (f32[32,12,32]{2,0,1:T(8,128)S(1)}, f32[32,12,32]{2,0,1:T(8,128)}, u32[]{:S(2)}) copy-start(f32[32,12,32]{2,0,1:T(8,128)} %copy-done.22) | copy-start | bytes 147460
  76.5 13.8 %collective-permute-start.2 = (bf16[2,128,1024]{2,1,0:T(8,128)(2,1)S(1)}, bf16[2,128,1024]{2,1,0:T(8,128)(2,1)}, u32[]{:S(2)}, u32[]{:S(2)}) collective-permute-start(bf16[2,128,1024]{2,1,0:T(8,128)(2,1)S(1)} %pad_maximum_fusion), channel_id=1, source_target_pairs={{0,4},{2,6},{4,0},{6,2},{8,12},{10,14},{12,8},{14,10},{16,20},{18,... | collective-permute-start | bytes 1572872 | tf_op jit(solution)/shard_map/ppermute | solution.py:501
  88.2 3.1 %copy-start.6 = (bf16[8,128,128]{2,1,0:T(8,128)(2,1)}, bf16[8,128,128]{2,1,0:T(8,128)(2,1)S(1)}, u32[]{:S(2)}) copy-start(bf16[8,128,128]{2,1,0:T(8,128)(2,1)S(1)} %attend.1) | copy-start | bytes 786436
  101.4 7.4 %copy-start.3 = (bf16[1,128,1024]{2,1,0:T(8,128)(2,1)S(1)}, bf16[1,128,1024]{2,1,0:T(8,128)(2,1)}, u32[]{:S(2)}) copy-start(bf16[1,128,1024]{2,1,0:T(8,128)(2,1)} %param.14) | copy-start | bytes 786436
  101.4 24.6 %collective-permute-start.3 = (bf16[4,2,2,32,1024]{4,3,2,1,0:T(8,128)(2,1)S(1)}, bf16[4,2,2,32,1024]{4,3,2,1,0:T(8,128)(2,1)}, u32[]{:S(2)}, u32[]{:S(2)}) collective-permute-start(bf16[4,2,2,32,1024]{4,3,2,1,0:T(8,128)(2,1)S(1)} %constant_dynamic-update-slice_fusion.kept), channel_id=1, source_target_pairs={{0,4},{2,6},{4,0},{6,2},{8,12},{10,14},{12,8},{14,10},{16,20},{18,... | collective-permute-start | bytes 3145736 | tf_op jit(solution)/shard_map/ppermute | solution.py:501
  102.8 29.4 %collective-permute-start.4 = (bf16[4,128,1024]{2,1,0:T(8,128)(2,1)S(1)}, bf16[4,128,1024]{2,1,0:T(8,128)(2,1)}, u32[]{:S(2)}, u32[]{:S(2)}) collective-permute-start(bf16[4,128,1024]{2,1,0:T(8,128)(2,1)S(1)} %constant_dynamic-update-slice_fusion.2.kept), channel_id=1, source_target_pairs={{0,1},{1,0},{2,3},{3,2},{4,5},{5,4},{6,7},{7,6},{8,9},{9,8},{10,11... | collective-permute-start | bytes 3145736 | tf_op jit(solution)/shard_map/ppermute | solution.py:508
  129.1 6.2 %copy-start.4 = (bf16[2,2,2,2,2,32,1024]{6,5,4,3,2,1,0:T(8,128)(2,1)}, bf16[2,2,2,2,2,32,1024]{6,5,4,3,2,1,0:T(8,128)(2,1)S(1)}, u32[]{:S(2)}) copy-start(bf16[2,2,2,2,2,32,1024]{6,5,4,3,2,1,0:T(8,128)(2,1)S(1)} %arrange.2) | copy-start | bytes 6291460
  154.8 3.0 %copy-start.18 = (bf16[1024,1024]{1,0:T(8,128)(2,1)}, bf16[1024,1024]{1,0:T(8,128)(2,1)S(1)}, u32[]{:S(2)}) copy-start(bf16[1024,1024]{1,0:T(8,128)(2,1)S(1)} %convolution_convert_fusion.1) | copy-start | bytes 6291460
  156.0 28.2 %collective-permute-start.5 = (bf16[2,1,2,128,1024]{4,3,2,1,0:T(8,128)(2,1)}, bf16[2,1,2,128,1024]{4,3,2,1,0:T(8,128)(2,1)}, u32[]{:S(2)}, u32[]{:S(2)}) collective-permute-start(bf16[2,1,2,128,1024]{4,3,2,1,0:T(8,128)(2,1)} %constant_dynamic-slice_fusion.6), channel_id=1, source_target_pairs={{0,4},{2,6},{4,0},{6,2},{8,12},{10,14},{12,8},{14,10},{16,20},{18,... | collective-permute-start | bytes 3145736 | tf_op jit(solution)/shard_map/ppermute | solution.py:501
  160.4 2.8 copy-start.12
  161.4 39.5 %collective-permute-start.6 = (bf16[2,2,2,2,1,32,1024]{6,5,3,1,4,2,0:T(8,128)(2,1)}, bf16[2,2,2,2,1,32,1024]{6,5,3,1,4,2,0:T(8,128)(2,1)}, u32[]{:S(2)}, u32[]{:S(2)}) collective-permute-start(bf16[2,2,2,2,1,32,1024]{6,5,3,1,4,2,0:T(8,128)(2,1)} %copy.34), channel_id=1, source_target_pairs={{0,1},{1,0},{2,3},{3,2},{4,5},{5,4},{6,7},{7,6},{8,9},{9,8},{10,11... | collective-permute-start | bytes 3145736 | tf_op jit(solution)/shard_map/ppermute | solution.py:508
  164.7 3.0 copy-start.8
  167.6 16.6 %copy-start.19 = (bf16[1024,1024]{1,0:T(8,128)(2,1)S(1)}, bf16[1024,1024]{1,0:T(8,128)(2,1)}, u32[]{:S(2)}) copy-start(bf16[1024,1024]{1,0:T(8,128)(2,1)} %copy-done.18) | copy-start | bytes 6291460
  184.2 4.2 %copy-start.25 = (bf16[2,2,2,32,1024]{4,3,2,1,0:T(8,128)(2,1)S(1)}, bf16[2,2,2,32,1024]{4,3,2,1,0:T(8,128)(2,1)}, u32[]{:S(2)}) copy-start(bf16[2,2,2,32,1024]{4,3,2,1,0:T(8,128)(2,1)} %get-tuple-element.61) | copy-start | bytes 1572868
  186.9 14.0 %copy-start.13 = (bf16[2,2,2,2,1,32,1024]{6,5,4,3,2,1,0:T(8,128)(2,1)S(1)}, bf16[2,2,2,2,1,32,1024]{6,5,4,3,2,1,0:T(8,128)(2,1)}, u32[]{:S(2)}) copy-start(bf16[2,2,2,2,1,32,1024]{6,5,4,3,2,1,0:T(8,128)(2,1)} %get-tuple-element.94) | copy-start | bytes 3145732
  187.7 16.0 %collective-permute-start.8 = (bf16[2,1,1,128,1024]{4,3,2,1,0:T(8,128)(2,1)}, bf16[2,1,1,128,1024]{4,3,2,1,0:T(8,128)(2,1)}, u32[]{:S(2)}, u32[]{:S(2)}) collective-permute-start(bf16[2,1,1,128,1024]{4,3,2,1,0:T(8,128)(2,1)} %constant_dynamic-slice_fusion.2), channel_id=1, source_target_pairs={{0,1},{1,0},{2,3},{3,2},{4,5},{5,4},{6,7},{7,6},{8,9},{9,8},{10,11... | collective-permute-start | bytes 1572872 | tf_op jit(solution)/shard_map/ppermute | solution.py:508
  200.9 2.8 copy-start.15
  202.7 3.1 %copy-start.1 = (bf16[2,2,2,384,128]{4,3,2,1,0:T(8,128)(2,1)S(1)}, bf16[2,2,2,384,128]{4,3,2,1,0:T(8,128)(2,1)}, u32[]{:S(2)}) copy-start(bf16[2,2,2,384,128]{4,3,2,1,0:T(8,128)(2,1)} %to_heads.2) | copy-start | bytes 2359300
  202.7 3.0 %copy-start.5 = (bf16[2,2,2,128,128]{4,3,2,1,0:T(8,128)(2,1)S(1)}, bf16[2,2,2,128,128]{4,3,2,1,0:T(8,128)(2,1)}, u32[]{:S(2)}) copy-start(bf16[2,2,2,128,128]{4,3,2,1,0:T(8,128)(2,1)} %to_heads.3) | copy-start | bytes 786436
  202.7 15.5 %collective-permute-start.7 = (bf16[2,2,1,2,1,32,1024]{6,5,3,1,4,2,0:T(8,128)(2,1)S(1)}, bf16[2,2,1,2,1,32,1024]{6,5,3,1,4,2,0:T(8,128)(2,1)S(1)}, u32[]{:S(2)}, u32[]{:S(2)}) collective-permute-start(bf16[2,2,1,2,1,32,1024]{6,5,3,1,4,2,0:T(8,128)(2,1)S(1)} %constant_dynamic-slice_fusion.3), channel_id=1, source_target_pairs={{0,4},{2,6},{4,0},{6,2},{8,12},{10,14},{12,8},{14,10},{16,20},{18,... | collective-permute-start | bytes 1572872 | tf_op jit(solution)/shard_map/ppermute | solution.py:501
  205.0 13.5 %collective-permute-start.9 = (bf16[1,1,128,1024]{3,2,1,0:T(8,128)(2,1)S(1)}, bf16[1,1,128,1024]{3,2,1,0:T(8,128)(2,1)S(1)}, u32[]{:S(2)}, u32[]{:S(2)}) collective-permute-start(bf16[1,1,128,1024]{3,2,1,0:T(8,128)(2,1)S(1)} %dynamic-slice_bitcast_fusion.1), channel_id=1, source_target_pairs={{0,16},{2,18},{4,20},{6,22},{8,24},{10,26},{12,28},{14,30},{16,0},... | collective-permute-start | bytes 786440 | tf_op jit(solution)/shard_map/ppermute | solution.py:501
  218.3 23.6 %copy-start.24 = (bf16[512,1024]{1,0:T(8,128)(2,1)S(1)}, bf16[512,1024]{1,0:T(8,128)(2,1)}, u32[]{:S(2)}) copy-start(bf16[512,1024]{1,0:T(8,128)(2,1)} %fusion.3) | copy-start | bytes 3145732
  241.8 13.7 %collective-permute-start.10 = (bf16[2,1,2,1,32,1024]{5,4,2,0,3,1:T(8,128)(2,1)S(1)}, bf16[2,1,2,1,32,1024]{5,4,2,0,3,1:T(8,128)(2,1)S(1)}, u32[]{:S(2)}, u32[]{:S(2)}) collective-permute-start(bf16[2,1,2,1,32,1024]{5,4,2,0,3,1:T(8,128)(2,1)S(1)} %dynamic-slice_bitcast_fusion), channel_id=1, source_target_pairs={{0,16},{2,18},{4,20},{6,22},{8,24},{10,26},{12,28},{14,30},{16,0},... | collective-permute-start | bytes 786440 | tf_op jit(solution)/shard_map/ppermute | solution.py:501
  244.2 2.6 copy-start.21
  255.6 36.0 %copy-start.10 = (bf16[128,1024]{1,0:T(8,128)(2,1)S(1)}, bf16[128,1024]{1,0:T(8,128)(2,1)}, u32[]{:S(2)}) copy-start(bf16[128,1024]{1,0:T(8,128)(2,1)} %copy-done.9) | copy-start | bytes 786436
  (12 other events, 17.9 us)
